TPU v7x, 512 devices: a whole 4x4x16 slice. The times are simulated.
512 devices in a mesh: gx: 16 (over z), gy: 4 (over x), gz: 8 (over y, core).
Axes of the slice: x: 4, y: 4, z: 16, core: 2. Of those that a mesh axis runs over, the one named last changes fastest.
Arguments:
- density: float32 [512, 64, 1024], P('gx', 'gy', 'gz'), may hold values from 0.5 to 2
- momentum: float32 [2, 512, 64, 1024], P(None, 'gx', 'gy', 'gz'), may hold values from -3 to 3
- lower_face: float32 [512], P('gx'), may hold values from 2048 to 8192
Outputs:
- updated: float32 [3, 512, 64, 1024], P(None, 'gx', 'gy', 'gz')
All inputs are finite; a program needn't handle non-finite values.
Results may differ from a plain program's by a relative error of at most 0.0003.
Values sent between devices are 32-bit elements; how exact they have to be, the bound alone decides.
A program may use at most 64 MiB of HBM per device.

v0:
```python
import jax
import jax.numpy as jnp
from jax import lax
from jax.sharding import PartitionSpec as P

time_step = 0.2


def passed_along(value, axis, steps):
    count = lax.axis_size(axis)
    first, last = (max(0, -steps), min(count, count - steps))
    return lax.ppermute(value, axis, [(source, source + steps) for source in range(first, last)])


def with_halo(block, sides, width):
    for axis, dim in sides:
        count = lax.axis_size(axis)
        forward = [(i, i + 1) for i in range(count - 1)]
        forward.append((count - 1, 0))
        backward = [(target, source) for source, target in forward]
        low = lax.ppermute(
            lax.slice_in_dim(block, block.shape[dim] - width, None, axis=dim), axis, forward
        )
        high = lax.ppermute(lax.slice_in_dim(block, 0, width, axis=dim), axis, backward)
        block = jnp.concatenate([low, block, high], axis=dim)
    return block


def central_sixth(padded, axis, count):

    def take(offset):
        return lax.slice_in_dim(padded, 3 + offset, 3 + offset + count, axis=axis)

    return (45.0 * (take(1) - take(-1)) - 9.0 * (take(2) - take(-2)) + (take(3) - take(-3))) / 60.0


def mat_mat(left, right):
    return jnp.einsum("nij,njk->nik", left, right, precision=lax.Precision.HIGHEST)


def mat_vec(left, vec):
    return jnp.einsum("nij,njab->niab", left, vec, precision=lax.Precision.HIGHEST)


def invert_pair(mat):
    det = mat[:, 0, 0] * mat[:, 1, 1] - mat[:, 0, 1] * mat[:, 1, 0]
    first = jnp.stack([mat[:, 1, 1], -mat[:, 0, 1]], -1)
    second = jnp.stack([-mat[:, 1, 0], mat[:, 0, 0]], -1)
    return jnp.stack([first, second], 1) / det[:, None, None]


def eliminate(current, lower_eq, upper_eq):
    rows, coup_lo, coup_hi = current
    eye_pair = jnp.eye(2, dtype=jnp.float32)[None]
    pivot = eye_pair - mat_mat(coup_lo, lower_eq[2]) - mat_mat(coup_hi, upper_eq[1])
    pivot_inv = invert_pair(pivot)
    new_rows = mat_vec(
        pivot_inv, rows + mat_vec(coup_lo, lower_eq[0]) + mat_vec(coup_hi, upper_eq[0])
    )
    new_lo = mat_mat(pivot_inv, mat_mat(coup_lo, lower_eq[1]))
    new_hi = mat_mat(pivot_inv, mat_mat(coup_hi, upper_eq[2]))
    return (new_rows, new_lo, new_hi)


def neighbours(payload, span):
    lower_eq = passed_along(payload, "gx", span)
    upper_eq = passed_along(payload, "gx", -span)
    return (lower_eq, upper_eq)


def on_device(density, momentum, lower_face):
    state = jnp.concatenate([density[None], momentum], 0)
    cells = state.shape[1]
    count_y = state.shape[2]
    count_z = state.shape[3]
    padded = with_halo(state, (("gy", 2), ("gz", 3)), 3)
    y_band = padded[:, :, :, 3 : 3 + count_z]
    z_band = padded[:, :, 3 : 3 + count_y, :]
    flux_y = y_band * (y_band[1] / y_band[0])[None]
    flux_z = z_band * (z_band[2] / z_band[0])[None]
    rhs = state - time_step * (
        central_sixth(flux_y, 2, count_y) + central_sixth(flux_z, 3, count_z)
    )
    position = lax.axis_index("gx")
    devices = lax.axis_size("gx")
    after = passed_along(lower_face[:1], "gx", -1)
    upper_last = jnp.where(position == devices - 1, lower_face[-1], after[0])
    upper = jnp.concatenate([lower_face[1:], upper_last[None]])
    diagonal = 1.0 + lower_face + upper
    block = jnp.diag(diagonal) - jnp.diag(lower_face[1:], -1) - jnp.diag(lower_face[1:], 1)
    factor = jnp.linalg.cholesky(block)
    inverse = jax.scipy.linalg.cho_solve((factor, True), jnp.eye(cells, dtype=jnp.float32))
    local = jnp.einsum("ij,kjab->kiab", inverse, rhs, precision=lax.Precision.HIGHEST)
    coup_left = lower_face[0]
    zero = jnp.zeros((), jnp.float32)
    first_a = coup_left * inverse[0, 0]
    first_b = upper_last * inverse[0, -1]
    last_a = coup_left * inverse[-1, 0]
    last_b = upper_last * inverse[-1, -1]
    coup_lo = jnp.stack([jnp.stack([zero, first_a]), jnp.stack([zero, last_a])])[None]
    coup_hi = jnp.stack([jnp.stack([first_b, zero]), jnp.stack([last_b, zero])])[None]
    rows = jnp.stack([local[:, 0], local[:, -1]], 0).reshape(1, 2, 3 * count_y, count_z)
    levels = (devices - 1).bit_length()
    current = (rows, coup_lo, coup_hi)
    for level in range(levels):
        lower_eq, upper_eq = neighbours(current, 1 << level)
        current = eliminate(current, lower_eq, upper_eq)
    lower_eq, upper_eq = neighbours((current[0],), 1)
    last_below = lower_eq[0][0, 1]
    first_above = upper_eq[0][0, 0]
    col_low = coup_left * inverse[:, 0]
    col_high = upper_last * inverse[:, -1]
    below_vals = last_below.reshape(3, 1, count_y, count_z)
    above_vals = first_above.reshape(3, 1, count_y, count_z)
    return (
        local
        + col_low[None, :, None, None] * below_vals
        + col_high[None, :, None, None] * above_vals
    )


def solution(mesh):
    placed = (P("gx", "gy", "gz"), P(None, "gx", "gy", "gz"), P("gx"))
    return jax.shard_map(
        on_device, mesh=mesh, in_specs=placed, out_specs=P(None, "gx", "gy", "gz"), check_vma=False
    )
```

profile of v0, /device:TPU:24, one launch (start us, length us, event | category | flops | bytes accessed | tf_op | source)
XLA Modules:
  0.0 205.0 jit_solution(4953659331570292331)
XLA Ops:
  0.0 1.2 fusion.23
  1.2 4.8 %collective-permute-start.1 = (f32[3,32,3,128]{3,1,2,0:T(8,128)S(1)}, f32[3,32,3,128]{3,1,2,0:T(8,128)S(1)}, u32[]{:S(2)}, u32[]{:S(2)}) collective-permute-start(f32[3,32,3,128]{3,1,2,0:T(8,128)S(1)} %copy.65), channel_id=1, source_target_pairs={{8,0},{16,8},{24,16},{0,24},{9,1},{17,9},{25,17},{1,25},{10,2},{18... | collective-permute-start | bytes 442376 | tf_op jit(solution)/shard_map/ppermute | solution.py:24
  6.1 1.9 collective-permute-start
  8.0 0.6 fusion.96
  8.6 1.3 collective-permute-start.4
  10.0 4.4 %collective-permute-done.4 = f32[1]{0:T(128)} collective-permute-done((f32[1]{0:T(128)}, f32[1]{0:T(128)}, u32[]{:S(2)}, u32[]{:S(2)}) %collective-permute-start.4) | collective-permute-done | bytes 36 | tf_op jit(solution)/shard_map/ppermute | solution.py:12
  15.8 2.9 %cholesky.17 = f32[32,32]{1,0:T(8,128)S(1)} custom-call(f32[32,32]{1,0:T(8,128)S(1)} %add_multiply_fusion), custom_call_target="Cholesky" | custom-call | tf_op jit(solution)/shard_map/jit(cholesky)/cholesky | solution.py:91
  18.8 0.6 compare_reduce_fusion
  19.4 0.7 fusion.34
  20.1 2.4 %custom-call.10 = f32[1,32,32]{1,2,0:T(8,128)S(1)} custom-call(f32[1,32,32]{2,1,0:T(8,128)S(1)} %fusion.34), custom_call_target="InvertDiagBlocksLowerTriangular" | custom-call | tf_op jit(solution)/shard_map/jit(_cho_solve)/triangular_solve | solution.py:92
  22.9 0.7 fusion.91
  26.2 1.3 collective-permute-start.6
  27.5 4.5 %collective-permute-start.7 = (f32[1,2,2]{2,1,0:T(2,128)S(1)}, f32[1,2,2]{2,1,0:T(2,128)S(1)}, u32[]{:S(2)}, u32[]{:S(2)}) collective-permute-start(f32[1,2,2]{2,1,0:T(2,128)S(1)} %fusion.88), channel_id=1, source_target_pairs={{0,32},{32,64},{64,96},{96,128},{128,160},{160,192},{192,224},{224... | collective-permute-start | bytes 56 | tf_op jit(solution)/shard_map/ppermute | solution.py:12
  33.4 3.8 %collective-permute-start.5 = (f32[1,2,2]{2,1,0:T(2,128)S(1)}, f32[1,2,2]{2,1,0:T(2,128)S(1)}, u32[]{:S(2)}, u32[]{:S(2)}) collective-permute-start(f32[1,2,2]{2,1,0:T(2,128)S(1)} %fusion.87), channel_id=1, source_target_pairs={{0,32},{32,64},{64,96},{96,128},{128,160},{160,192},{192,224},{224... | collective-permute-start | bytes 56 | tf_op jit(solution)/shard_map/ppermute | solution.py:12
  37.2 1.3 collective-permute-start.8
  38.8 0.7 fusion.95
  43.4 1.4 maximum_divide_fusion.1
  45.0 1.3 collective-permute-start.10
  46.3 8.9 %collective-permute-start.11 = (f32[1,2,2]{2,1,0:T(2,128)S(1)}, f32[1,2,2]{2,1,0:T(2,128)S(1)}, u32[]{:S(2)}, u32[]{:S(2)}) collective-permute-start(f32[1,2,2]{2,1,0:T(2,128)S(1)} %bitcast.246), channel_id=1, source_target_pairs={{0,64},{32,96},{64,128},{96,160},{128,192},{160,224},{192,256},{22... | collective-permute-start | bytes 56 | tf_op jit(solution)/shard_map/ppermute | solution.py:12
  55.4 6.0 %collective-permute-start.9 = (f32[1,2,2]{2,1,0:T(2,128)S(1)}, f32[1,2,2]{2,1,0:T(2,128)S(1)}, u32[]{:S(2)}, u32[]{:S(2)}) collective-permute-start(f32[1,2,2]{2,1,0:T(2,128)S(1)} %bitcast.247), channel_id=1, source_target_pairs={{0,64},{32,96},{64,128},{96,160},{128,192},{160,224},{192,256},{22... | collective-permute-start | bytes 56 | tf_op jit(solution)/shard_map/ppermute | solution.py:12
  61.5 1.3 collective-permute-start.12
  63.0 0.7 fusion.94
  67.5 1.4 maximum_divide_fusion.2
  69.2 1.3 collective-permute-start.14
  70.5 10.4 %collective-permute-start.15 = (f32[1,2,2]{2,1,0:T(2,128)S(1)}, f32[1,2,2]{2,1,0:T(2,128)S(1)}, u32[]{:S(2)}, u32[]{:S(2)}) collective-permute-start(f32[1,2,2]{2,1,0:T(2,128)S(1)} %bitcast.250), channel_id=1, source_target_pairs={{0,128},{32,160},{64,192},{96,224},{128,256},{160,288},{192,320},{... | collective-permute-start | bytes 56 | tf_op jit(solution)/shard_map/ppermute | solution.py:12
  81.1 7.8 %collective-permute-start.13 = (f32[1,2,2]{2,1,0:T(2,128)S(1)}, f32[1,2,2]{2,1,0:T(2,128)S(1)}, u32[]{:S(2)}, u32[]{:S(2)}) collective-permute-start(f32[1,2,2]{2,1,0:T(2,128)S(1)} %bitcast.251), channel_id=1, source_target_pairs={{0,128},{32,160},{64,192},{96,224},{128,256},{160,288},{192,320},{... | collective-permute-start | bytes 56 | tf_op jit(solution)/shard_map/ppermute | solution.py:12
  89.0 1.3 collective-permute-start.16
  90.6 0.7 fusion.93
  95.0 1.3 maximum_divide_fusion.3
  96.5 0.7 fusion.101
  97.2 1.1 collective-permute-done.16
  98.4 0.7 fusion.58
  100.0 0.8 fusion.22
  100.8 1.2 copy.52
  102.0 1.2 copy.51
  103.8 0.8 collective-permute-done.3
  104.6 1.4 copy.54
  106.0 1.6 collective-permute-done.2
  107.6 2.5 %copy.53 = f32[3,32,22,3]{3,2,1,0:T(8,128)} copy(f32[3,32,22,3]{1,2,3,0:T(8,128)} %collective-permute-done.2) | data formatting | bytes 50688 | tf_op jit(solution)/shard_map/ppermute | solution.py:21
  110.1 2.8 %pad_maximum_fusion = f32[3,32,22,134]{3,2,1,0:T(8,128)S(1)} fusion(f32[3,32,22,3]{3,2,1,0:T(8,128)S(1)} %copy.54, f32[3,32,3,128]{3,2,1,0:T(4,128)S(1)} %copy.50, f32[2,32,16,128]{3,2,1,0:T(8,128)S(1)} %copy-done, f32[1,32,16,128]{3,2,1,0:T(8,128)S(1)} %bitcast.230, f32[3,32,3,128]{3,2,1,0:T(4,128)S(1)} %copy.49, f32[3,32,22,3]{3,2,1,0:T(8,128)} %copy.53), kind=kLoop, calls=%fused_computation | loop fusion | flops 1415040 | bytes 2264064 | tf_op jit(solution)/shard_map/concatenate | solution.py:25
  112.8 0.6 fusion.21
  113.8 1.1 fusion.9
  115.0 1.0 convolution_bitcast_fusion
  116.2 1.3 collective-permute-start.20
  117.7 1.3 collective-permute-start.18
  119.0 14.4 %collective-permute-start.17 = (f32[1,2,2]{2,1,0:T(2,128)S(1)}, f32[1,2,2]{2,1,0:T(2,128)S(1)}, u32[]{:S(2)}, u32[]{:S(2)}) collective-permute-start(f32[1,2,2]{2,1,0:T(2,128)S(1)} %bitcast.254), channel_id=1, source_target_pairs={{0,256},{32,288},{64,320},{96,352},{128,384},{160,416},{192,448},{... | collective-permute-start | bytes 56 | tf_op jit(solution)/shard_map/ppermute | solution.py:12
  133.4 3.4 %collective-permute-start.19 = (f32[1,2,48,128]{3,1,2,0:T(2,128)S(1)}, f32[1,2,48,128]{3,1,2,0:T(2,128)S(1)}, u32[]{:S(2)}, u32[]{:S(2)}) collective-permute-start(f32[1,2,48,128]{3,1,2,0:T(2,128)S(1)} %pad_maximum_fusion.3), channel_id=1, source_target_pairs={{0,32},{32,64},{64,96},{96,128},{128,160},{160,192},{192,224},{224... | collective-permute-start | bytes 147464 | tf_op jit(solution)/shard_map/ppermute | solution.py:12
  137.1 1.4 collective-permute-done.19
  139.2 5.7 %collective-permute-start.21 = (f32[1,2,48,128]{3,1,2,0:T(2,128)S(1)}, f32[1,2,48,128]{3,1,2,0:T(2,128)S(1)}, u32[]{:S(2)}, u32[]{:S(2)}) collective-permute-start(f32[1,2,48,128]{3,1,2,0:T(2,128)S(1)} %bitcast.243), channel_id=1, source_target_pairs={{0,64},{32,96},{64,128},{96,160},{128,192},{160,224},{192,256},{22... | collective-permute-start | bytes 147464 | tf_op jit(solution)/shard_map/ppermute | solution.py:12
  145.0 1.3 collective-permute-start.22
  146.9 7.6 %collective-permute-done.22 = f32[1,2,48,128]{3,1,2,0:T(2,128)S(1)} collective-permute-done((f32[1,2,48,128]{3,1,2,0:T(2,128)S(1)}, f32[1,2,48,128]{3,1,2,0:T(2,128)S(1)}, u32[]{:S(2)}, u32[]{:S(2)}) %collective-permute-start.22) | collective-permute-done | bytes 49184 | tf_op jit(solution)/shard_map/ppermute | solution.py:12
  155.2 4.9 %collective-permute-start.23 = (f32[1,2,48,128]{3,1,2,0:T(2,128)S(1)}, f32[1,2,48,128]{3,1,2,0:T(2,128)S(1)}, u32[]{:S(2)}, u32[]{:S(2)}) collective-permute-start(f32[1,2,48,128]{3,1,2,0:T(2,128)S(1)} %bitcast.241), channel_id=1, source_target_pairs={{0,128},{32,160},{64,192},{96,224},{128,256},{160,288},{192,320},{... | collective-permute-start | bytes 147464 | tf_op jit(solution)/shard_map/ppermute | solution.py:12
  160.2 1.3 collective-permute-start.24
  162.1 9.2 %collective-permute-done.24 = f32[1,2,48,128]{3,1,2,0:T(2,128)S(1)} collective-permute-done((f32[1,2,48,128]{3,1,2,0:T(2,128)S(1)}, f32[1,2,48,128]{3,1,2,0:T(2,128)S(1)}, u32[]{:S(2)}, u32[]{:S(2)}) %collective-permute-start.24) | collective-permute-done | bytes 49184 | tf_op jit(solution)/shard_map/ppermute | solution.py:12
  172.0 2.6 %collective-permute-start.25 = (f32[1,2,48,128]{3,1,2,0:T(2,128)S(1)}, f32[1,2,48,128]{3,1,2,0:T(2,128)S(1)}, u32[]{:S(2)}, u32[]{:S(2)}) collective-permute-start(f32[1,2,48,128]{3,1,2,0:T(2,128)S(1)} %bitcast.239), channel_id=1, source_target_pairs={{0,256},{32,288},{64,320},{96,352},{128,384},{160,416},{192,448},{... | collective-permute-start | bytes 147464 | tf_op jit(solution)/shard_map/ppermute | solution.py:12
  174.6 0.6 fusion.92
  179.1 1.3 collective-permute-start.26
  180.8 13.1 %collective-permute-done.26 = f32[1,2,48,128]{3,1,2,0:T(2,128)S(1)} collective-permute-done((f32[1,2,48,128]{3,1,2,0:T(2,128)S(1)}, f32[1,2,48,128]{3,1,2,0:T(2,128)S(1)}, u32[]{:S(2)}, u32[]{:S(2)}) %collective-permute-start.26) | collective-permute-done | bytes 49184 | tf_op jit(solution)/shard_map/ppermute | solution.py:12
  194.2 1.7 convolution_bitcast_fusion.1
  195.8 1.3 collective-permute-start.28
  197.1 4.5 %collective-permute-start.27 = (f32[1,2,48,128]{3,1,2,0:T(2,128)S(1)}, f32[1,2,48,128]{3,1,2,0:T(2,128)S(1)}, u32[]{:S(2)}, u32[]{:S(2)}) collective-permute-start(f32[1,2,48,128]{3,1,2,0:T(2,128)S(1)} %convolution_bitcast_fusion.1), channel_id=1, source_target_pairs={{0,32},{32,64},{64,96},{96,128},{128,160},{160,192},{192,224},{224... | collective-permute-start | bytes 147464 | tf_op jit(solution)/shard_map/ppermute | solution.py:12
  201.7 0.6 fusion.84
  202.4 1.1 collective-permute-done.27
  203.7 1.3 copy.61
  (134 shorter events, 9.5 us)
Async XLA Ops:
  0.0 8.0 %copy-start.8 = (f32[32]{0:T(128)S(1)}, f32[32]{0:T(128)}, u32[]{:S(2)}) copy-start(f32[32]{0:T(128)} %param.5) | copy-start | bytes 388
  1.2 98.2 %copy-start = (f32[2,32,16,128]{3,2,1,0:T(8,128)S(1)}, f32[2,32,16,128]{3,2,1,0:T(8,128)}, u32[]{:S(2)}) copy-start(f32[2,32,16,128]{3,2,1,0:T(8,128)} %param.4) | copy-start | bytes 1572868
  1.2 98.2 %copy-start.2 = (f32[32,16,128]{2,1,0:T(8,128)S(1)}, f32[32,16,128]{2,1,0:T(8,128)}, u32[]{:S(2)}) copy-start(f32[32,16,128]{2,1,0:T(8,128)} %param.3) | copy-start | bytes 786436
  1.2 97.9 %collective-permute-start.1 = (f32[3,32,3,128]{3,1,2,0:T(8,128)S(1)}, f32[3,32,3,128]{3,1,2,0:T(8,128)S(1)}, u32[]{:S(2)}, u32[]{:S(2)}) collective-permute-start(f32[3,32,3,128]{3,1,2,0:T(8,128)S(1)} %copy.65), channel_id=1, source_target_pairs={{8,0},{16,8},{24,16},{0,24},{9,1},{17,9},{25,17},{1,25},{10,2},{18... | collective-permute-start | bytes 442376 | tf_op jit(solution)/shard_map/ppermute | solution.py:24
  6.1 93.2 %collective-permute-start = (f32[3,32,3,128]{3,1,2,0:T(8,128)S(1)}, f32[3,32,3,128]{3,1,2,0:T(8,128)S(1)}, u32[]{:S(2)}, u32[]{:S(2)}) collective-permute-start(f32[3,32,3,128]{3,1,2,0:T(8,128)S(1)} %copy.64), channel_id=1, source_target_pairs={{0,8},{8,16},{16,24},{24,0},{1,9},{9,17},{17,25},{25,1},{2,10},{10... | collective-permute-start | bytes 442376 | tf_op jit(solution)/shard_map/ppermute | solution.py:21
  8.6 5.8 %collective-permute-start.4 = (f32[1]{0:T(128)}, f32[1]{0:T(128)}, u32[]{:S(2)}, u32[]{:S(2)}) collective-permute-start(f32[1]{0:T(128)} %get-tuple-element.36), channel_id=1, source_target_pairs={{32,0},{64,32},{96,64},{128,96},{160,128},{192,160},{224,192},{256... | collective-permute-start | bytes 20 | tf_op jit(solution)/shard_map/ppermute | solution.py:12
  26.2 72.9 %copy-start.9 = (f32[1,2]{1,0:T(1,128)}, f32[1,2]{1,0:T(1,128)S(1)}, u32[]{:S(2)}) copy-start(f32[1,2]{1,0:T(1,128)S(1)} %get-tuple-element.40) | copy-start | bytes 28
  26.2 72.9 %copy-start.11 = (f32[1,2]{1,0:T(1,128)}, f32[1,2]{1,0:T(1,128)S(1)}, u32[]{:S(2)}) copy-start(f32[1,2]{1,0:T(1,128)S(1)} %get-tuple-element.41) | copy-start | bytes 28
  26.2 11.0 %collective-permute-start.6 = (f32[1,2,2]{2,1,0:T(2,128)S(1)}, f32[1,2,2]{2,1,0:T(2,128)S(1)}, u32[]{:S(2)}, u32[]{:S(2)}) collective-permute-start(f32[1,2,2]{2,1,0:T(2,128)S(1)} %fusion.88), channel_id=1, source_target_pairs={{32,0},{64,32},{96,64},{128,96},{160,128},{192,160},{224,192},{256... | collective-permute-start | bytes 56 | tf_op jit(solution)/shard_map/ppermute | solution.py:12
  27.5 17.2 %collective-permute-start.7 = (f32[1,2,2]{2,1,0:T(2,128)S(1)}, f32[1,2,2]{2,1,0:T(2,128)S(1)}, u32[]{:S(2)}, u32[]{:S(2)}) collective-permute-start(f32[1,2,2]{2,1,0:T(2,128)S(1)} %fusion.88), channel_id=1, source_target_pairs={{0,32},{32,64},{64,96},{96,128},{128,160},{160,192},{192,224},{224... | collective-permute-start | bytes 56 | tf_op jit(solution)/shard_map/ppermute | solution.py:12
  33.4 65.7 %copy-start.4 = (f32[1,2]{1,0:T(1,128)}, f32[1,2]{1,0:T(1,128)S(1)}, u32[]{:S(2)}) copy-start(f32[1,2]{1,0:T(1,128)S(1)} %get-tuple-element.38) | copy-start | bytes 28
  33.4 65.7 %copy-start.6 = (f32[1,2]{1,0:T(1,128)}, f32[1,2]{1,0:T(1,128)S(1)}, u32[]{:S(2)}) copy-start(f32[1,2]{1,0:T(1,128)S(1)} %get-tuple-element.39) | copy-start | bytes 28
  33.4 5.3 %collective-permute-start.5 = (f32[1,2,2]{2,1,0:T(2,128)S(1)}, f32[1,2,2]{2,1,0:T(2,128)S(1)}, u32[]{:S(2)}, u32[]{:S(2)}) collective-permute-start(f32[1,2,2]{2,1,0:T(2,128)S(1)} %fusion.87), channel_id=1, source_target_pairs={{0,32},{32,64},{64,96},{96,128},{128,160},{160,192},{192,224},{224... | collective-permute-start | bytes 56 | tf_op jit(solution)/shard_map/ppermute | solution.py:12
  37.2 17.9 %collective-permute-start.8 = (f32[1,2,2]{2,1,0:T(2,128)S(1)}, f32[1,2,2]{2,1,0:T(2,128)S(1)}, u32[]{:S(2)}, u32[]{:S(2)}) collective-permute-start(f32[1,2,2]{2,1,0:T(2,128)S(1)} %fusion.87), channel_id=1, source_target_pairs={{32,0},{64,32},{96,64},{128,96},{160,128},{192,160},{224,192},{256... | collective-permute-start | bytes 56 | tf_op jit(solution)/shard_map/ppermute | solution.py:12
  44.7 54.4 %copy-start.13 = (f32[2,2]{1,0:T(2,128)}, f32[2,2]{1,0:T(2,128)S(1)}, u32[]{:S(2)}) copy-start(f32[2,2]{1,0:T(2,128)S(1)} %maximum_divide_fusion.1) | copy-start | bytes 52
  45.0 54.1 %copy-start.19 = (f32[2,2]{1,0:T(2,128)}, f32[2,2]{1,0:T(2,128)S(1)}, u32[]{:S(2)}) copy-start(f32[2,2]{1,0:T(2,128)S(1)} %fusion.97) | copy-start | bytes 52
  45.0 16.5 %collective-permute-start.10 = (f32[1,2,2]{2,1,0:T(2,128)S(1)}, f32[1,2,2]{2,1,0:T(2,128)S(1)}, u32[]{:S(2)}, u32[]{:S(2)}) collective-permute-start(f32[1,2,2]{2,1,0:T(2,128)S(1)} %bitcast.245), channel_id=1, source_target_pairs={{64,0},{96,32},{128,64},{160,96},{192,128},{224,160},{256,192},{28... | collective-permute-start | bytes 56 | tf_op jit(solution)/shard_map/ppermute | solution.py:12
  46.3 22.6 %collective-permute-start.11 = (f32[1,2,2]{2,1,0:T(2,128)S(1)}, f32[1,2,2]{2,1,0:T(2,128)S(1)}, u32[]{:S(2)}, u32[]{:S(2)}) collective-permute-start(f32[1,2,2]{2,1,0:T(2,128)S(1)} %bitcast.246), channel_id=1, source_target_pairs={{0,64},{32,96},{64,128},{96,160},{128,192},{160,224},{192,256},{22... | collective-permute-start | bytes 56 | tf_op jit(solution)/shard_map/ppermute | solution.py:12
  55.4 35.0 %copy-start.21 = (f32[2,2]{1,0:T(2,128)}, f32[2,2]{1,0:T(2,128)S(1)}, u32[]{:S(2)}) copy-start(f32[2,2]{1,0:T(2,128)S(1)} %fusion.98) | copy-start | bytes 52
  55.4 7.5 %collective-permute-start.9 = (f32[1,2,2]{2,1,0:T(2,128)S(1)}, f32[1,2,2]{2,1,0:T(2,128)S(1)}, u32[]{:S(2)}, u32[]{:S(2)}) collective-permute-start(f32[1,2,2]{2,1,0:T(2,128)S(1)} %bitcast.247), channel_id=1, source_target_pairs={{0,64},{32,96},{64,128},{96,160},{128,192},{160,224},{192,256},{22... | collective-permute-start | bytes 56 | tf_op jit(solution)/shard_map/ppermute | solution.py:12
  61.5 19.4 %collective-permute-start.12 = (f32[1,2,2]{2,1,0:T(2,128)S(1)}, f32[1,2,2]{2,1,0:T(2,128)S(1)}, u32[]{:S(2)}, u32[]{:S(2)}) collective-permute-start(f32[1,2,2]{2,1,0:T(2,128)S(1)} %bitcast.248), channel_id=1, source_target_pairs={{64,0},{96,32},{128,64},{160,96},{192,128},{224,160},{256,192},{28... | collective-permute-start | bytes 56 | tf_op jit(solution)/shard_map/ppermute | solution.py:12
  68.9 30.2 %copy-start.15 = (f32[2,2]{1,0:T(2,128)}, f32[2,2]{1,0:T(2,128)S(1)}, u32[]{:S(2)}) copy-start(f32[2,2]{1,0:T(2,128)S(1)} %maximum_divide_fusion.2) | copy-start | bytes 52
  69.2 29.9 %copy-start.23 = (f32[2,2]{1,0:T(2,128)}, f32[2,2]{1,0:T(2,128)S(1)}, u32[]{:S(2)}) copy-start(f32[2,2]{1,0:T(2,128)S(1)} %fusion.99) | copy-start | bytes 52
  69.2 19.8 %collective-permute-start.14 = (f32[1,2,2]{2,1,0:T(2,128)S(1)}, f32[1,2,2]{2,1,0:T(2,128)S(1)}, u32[]{:S(2)}, u32[]{:S(2)}) collective-permute-start(f32[1,2,2]{2,1,0:T(2,128)S(1)} %bitcast.249), channel_id=1, source_target_pairs={{128,0},{160,32},{192,64},{224,96},{256,128},{288,160},{320,192},{... | collective-permute-start | bytes 56 | tf_op jit(solution)/shard_map/ppermute | solution.py:12
  70.5 25.9 %collective-permute-start.15 = (f32[1,2,2]{2,1,0:T(2,128)S(1)}, f32[1,2,2]{2,1,0:T(2,128)S(1)}, u32[]{:S(2)}, u32[]{:S(2)}) collective-permute-start(f32[1,2,2]{2,1,0:T(2,128)S(1)} %bitcast.250), channel_id=1, source_target_pairs={{0,128},{32,160},{64,192},{96,224},{128,256},{160,288},{192,320},{... | collective-permute-start | bytes 56 | tf_op jit(solution)/shard_map/ppermute | solution.py:12
  81.1 18.0 %copy-start.25 = (f32[2,2]{1,0:T(2,128)}, f32[2,2]{1,0:T(2,128)S(1)}, u32[]{:S(2)}) copy-start(f32[2,2]{1,0:T(2,128)S(1)} %fusion.100) | copy-start | bytes 52
  81.1 9.3 %collective-permute-start.13 = (f32[1,2,2]{2,1,0:T(2,128)S(1)}, f32[1,2,2]{2,1,0:T(2,128)S(1)}, u32[]{:S(2)}, u32[]{:S(2)}) collective-permute-start(f32[1,2,2]{2,1,0:T(2,128)S(1)} %bitcast.251), channel_id=1, source_target_pairs={{0,128},{32,160},{64,192},{96,224},{128,256},{160,288},{192,320},{... | collective-permute-start | bytes 56 | tf_op jit(solution)/shard_map/ppermute | solution.py:12
  89.0 9.4 %collective-permute-start.16 = (f32[1,2,2]{2,1,0:T(2,128)S(1)}, f32[1,2,2]{2,1,0:T(2,128)S(1)}, u32[]{:S(2)}, u32[]{:S(2)}) collective-permute-start(f32[1,2,2]{2,1,0:T(2,128)S(1)} %bitcast.252), channel_id=1, source_target_pairs={{128,0},{160,32},{192,64},{224,96},{256,128},{288,160},{320,192},{... | collective-permute-start | bytes 56 | tf_op jit(solution)/shard_map/ppermute | solution.py:12
  96.4 2.8 %copy-start.17 = (f32[2,2]{1,0:T(2,128)}, f32[2,2]{1,0:T(2,128)S(1)}, u32[]{:S(2)}) copy-start(f32[2,2]{1,0:T(2,128)S(1)} %maximum_divide_fusion.3) | copy-start | bytes 52
  102.0 1.7 copy-start.3
  102.0 2.6 %collective-permute-start.3 = (f32[3,32,22,3]{1,2,3,0:T(8,128)}, f32[3,32,22,3]{1,2,3,0:T(8,128)}, u32[]{:S(2)}, u32[]{:S(2)}) collective-permute-start(f32[3,32,22,3]{1,2,3,0:T(8,128)} %copy.52), channel_id=1, source_target_pairs={{1,0},{2,1},{3,2},{4,3},{5,4},{6,5},{7,6},{0,7},{9,8},{10,9},{11,1... | collective-permute-start | bytes 76040 | tf_op jit(solution)/shard_map/ppermute | solution.py:24
  103.1 4.5 %collective-permute-start.2 = (f32[3,32,22,3]{1,2,3,0:T(8,128)}, f32[3,32,22,3]{1,2,3,0:T(8,128)}, u32[]{:S(2)}, u32[]{:S(2)}) collective-permute-start(f32[3,32,22,3]{1,2,3,0:T(8,128)} %copy.51), channel_id=1, source_target_pairs={{0,1},{1,2},{2,3},{3,4},{4,5},{5,6},{6,7},{7,0},{8,9},{9,10},{10,1... | collective-permute-start | bytes 76040 | tf_op jit(solution)/shard_map/ppermute | solution.py:21
  110.1 2.8 %copy-start.1 = (f32[3,32,22,3]{3,2,1,0:T(8,128)S(1)}, f32[3,32,22,3]{3,2,1,0:T(8,128)}, u32[]{:S(2)}) copy-start(f32[3,32,22,3]{3,2,1,0:T(8,128)} %copy.53) | copy-start | bytes 76036
  114.9 2.6 %copy-start.18 = (f32[2,2]{1,0:T(2,128)S(1)}, f32[2,2]{1,0:T(2,128)}, u32[]{:S(2)}) copy-start(f32[2,2]{1,0:T(2,128)} %copy-done.17) | copy-start | bytes 52
  114.9 2.6 %copy-start.28 = (f32[2,2]{1,0:T(2,128)S(1)}, f32[2,2]{1,0:T(2,128)}, u32[]{:S(2)}) copy-start(f32[2,2]{1,0:T(2,128)} %fusion.58) | copy-start | bytes 52
  114.9 2.7 %copy-start.27 = (f32[2,2]{1,0:T(2,128)S(1)}, f32[2,2]{1,0:T(2,128)}, u32[]{:S(2)}) copy-start(f32[2,2]{1,0:T(2,128)} %fusion.101) | copy-start | bytes 52
  114.9 21.8 %copy-start.5 = (f32[1,2]{1,0:T(1,128)S(1)}, f32[1,2]{1,0:T(1,128)}, u32[]{:S(2)}) copy-start(f32[1,2]{1,0:T(1,128)} %copy-done.4) | copy-start | bytes 28
  115.0 21.8 %copy-start.7 = (f32[1,2]{1,0:T(1,128)S(1)}, f32[1,2]{1,0:T(1,128)}, u32[]{:S(2)}) copy-start(f32[1,2]{1,0:T(1,128)} %copy-done.6) | copy-start | bytes 28
  115.0 23.5 %copy-start.10 = (f32[1,2]{1,0:T(1,128)S(1)}, f32[1,2]{1,0:T(1,128)}, u32[]{:S(2)}) copy-start(f32[1,2]{1,0:T(1,128)} %copy-done.9) | copy-start | bytes 28
  115.0 23.5 %copy-start.12 = (f32[1,2]{1,0:T(1,128)S(1)}, f32[1,2]{1,0:T(1,128)}, u32[]{:S(2)}) copy-start(f32[1,2]{1,0:T(1,128)} %copy-done.11) | copy-start | bytes 28
  115.0 23.8 %copy-start.14 = (f32[2,2]{1,0:T(2,128)S(1)}, f32[2,2]{1,0:T(2,128)}, u32[]{:S(2)}) copy-start(f32[2,2]{1,0:T(2,128)} %copy-done.13) | copy-start | bytes 52
  115.0 31.6 %copy-start.20 = (f32[2,2]{1,0:T(2,128)S(1)}, f32[2,2]{1,0:T(2,128)}, u32[]{:S(2)}) copy-start(f32[2,2]{1,0:T(2,128)} %copy-done.19) | copy-start | bytes 52
  115.0 39.5 %copy-start.22 = (f32[2,2]{1,0:T(2,128)S(1)}, f32[2,2]{1,0:T(2,128)}, u32[]{:S(2)}) copy-start(f32[2,2]{1,0:T(2,128)} %copy-done.21) | copy-start | bytes 52
  115.0 39.8 %copy-start.16 = (f32[2,2]{1,0:T(2,128)S(1)}, f32[2,2]{1,0:T(2,128)}, u32[]{:S(2)}) copy-start(f32[2,2]{1,0:T(2,128)} %copy-done.15) | copy-start | bytes 52
  115.0 46.8 %copy-start.24 = (f32[2,2]{1,0:T(2,128)S(1)}, f32[2,2]{1,0:T(2,128)}, u32[]{:S(2)}) copy-start(f32[2,2]{1,0:T(2,128)} %copy-done.23) | copy-start | bytes 52
  115.0 56.3 %copy-start.26 = (f32[2,2]{1,0:T(2,128)S(1)}, f32[2,2]{1,0:T(2,128)}, u32[]{:S(2)}) copy-start(f32[2,2]{1,0:T(2,128)} %copy-done.25) | copy-start | bytes 52
  116.2 20.6 %collective-permute-start.20 = (f32[1,2,48,128]{3,1,2,0:T(2,128)S(1)}, f32[1,2,48,128]{3,1,2,0:T(2,128)S(1)}, u32[]{:S(2)}, u32[]{:S(2)}) collective-permute-start(f32[1,2,48,128]{3,1,2,0:T(2,128)S(1)} %pad_maximum_fusion.3), channel_id=1, source_target_pairs={{32,0},{64,32},{96,64},{128,96},{160,128},{192,160},{224,192},{256... | collective-permute-start | bytes 147464 | tf_op jit(solution)/shard_map/ppermute | solution.py:12
  117.7 27.2 %collective-permute-start.18 = (f32[1,2,2]{2,1,0:T(2,128)S(1)}, f32[1,2,2]{2,1,0:T(2,128)S(1)}, u32[]{:S(2)}, u32[]{:S(2)}) collective-permute-start(f32[1,2,2]{2,1,0:T(2,128)S(1)} %bitcast.253), channel_id=1, source_target_pairs={{256,0},{288,32},{320,64},{352,96},{384,128},{416,160},{448,192},{... | collective-permute-start | bytes 56 | tf_op jit(solution)/shard_map/ppermute | solution.py:12
  119.0 41.1 %collective-permute-start.17 = (f32[1,2,2]{2,1,0:T(2,128)S(1)}, f32[1,2,2]{2,1,0:T(2,128)S(1)}, u32[]{:S(2)}, u32[]{:S(2)}) collective-permute-start(f32[1,2,2]{2,1,0:T(2,128)S(1)} %bitcast.254), channel_id=1, source_target_pairs={{0,256},{32,288},{64,320},{96,352},{128,384},{160,416},{192,448},{... | collective-permute-start | bytes 56 | tf_op jit(solution)/shard_map/ppermute | solution.py:12
  133.4 5.2 %collective-permute-start.19 = (f32[1,2,48,128]{3,1,2,0:T(2,128)S(1)}, f32[1,2,48,128]{3,1,2,0:T(2,128)S(1)}, u32[]{:S(2)}, u32[]{:S(2)}) collective-permute-start(f32[1,2,48,128]{3,1,2,0:T(2,128)S(1)} %pad_maximum_fusion.3), channel_id=1, source_target_pairs={{0,32},{32,64},{64,96},{96,128},{128,160},{160,192},{192,224},{224... | collective-permute-start | bytes 147464 | tf_op jit(solution)/shard_map/ppermute | solution.py:12
  139.2 7.4 %collective-permute-start.21 = (f32[1,2,48,128]{3,1,2,0:T(2,128)S(1)}, f32[1,2,48,128]{3,1,2,0:T(2,128)S(1)}, u32[]{:S(2)}, u32[]{:S(2)}) collective-permute-start(f32[1,2,48,128]{3,1,2,0:T(2,128)S(1)} %bitcast.243), channel_id=1, source_target_pairs={{0,64},{32,96},{64,128},{96,160},{128,192},{160,224},{192,256},{22... | collective-permute-start | bytes 147464 | tf_op jit(solution)/shard_map/ppermute | solution.py:12
  145.0 9.5 %collective-permute-start.22 = (f32[1,2,48,128]{3,1,2,0:T(2,128)S(1)}, f32[1,2,48,128]{3,1,2,0:T(2,128)S(1)}, u32[]{:S(2)}, u32[]{:S(2)}) collective-permute-start(f32[1,2,48,128]{3,1,2,0:T(2,128)S(1)} %bitcast.244), channel_id=1, source_target_pairs={{64,0},{96,32},{128,64},{160,96},{192,128},{224,160},{256,192},{28... | collective-permute-start | bytes 147464 | tf_op jit(solution)/shard_map/ppermute | solution.py:12
  155.2 6.7 %collective-permute-start.23 = (f32[1,2,48,128]{3,1,2,0:T(2,128)S(1)}, f32[1,2,48,128]{3,1,2,0:T(2,128)S(1)}, u32[]{:S(2)}, u32[]{:S(2)}) collective-permute-start(f32[1,2,48,128]{3,1,2,0:T(2,128)S(1)} %bitcast.241), channel_id=1, source_target_pairs={{0,128},{32,160},{64,192},{96,224},{128,256},{160,288},{192,320},{... | collective-permute-start | bytes 147464 | tf_op jit(solution)/shard_map/ppermute | solution.py:12
  160.2 11.1 %collective-permute-start.24 = (f32[1,2,48,128]{3,1,2,0:T(2,128)S(1)}, f32[1,2,48,128]{3,1,2,0:T(2,128)S(1)}, u32[]{:S(2)}, u32[]{:S(2)}) collective-permute-start(f32[1,2,48,128]{3,1,2,0:T(2,128)S(1)} %bitcast.242), channel_id=1, source_target_pairs={{128,0},{160,32},{192,64},{224,96},{256,128},{288,160},{320,192},{... | collective-permute-start | bytes 147464 | tf_op jit(solution)/shard_map/ppermute | solution.py:12
  172.0 8.5 %collective-permute-start.25 = (f32[1,2,48,128]{3,1,2,0:T(2,128)S(1)}, f32[1,2,48,128]{3,1,2,0:T(2,128)S(1)}, u32[]{:S(2)}, u32[]{:S(2)}) collective-permute-start(f32[1,2,48,128]{3,1,2,0:T(2,128)S(1)} %bitcast.239), channel_id=1, source_target_pairs={{0,256},{32,288},{64,320},{96,352},{128,384},{160,416},{192,448},{... | collective-permute-start | bytes 147464 | tf_op jit(solution)/shard_map/ppermute | solution.py:12
  179.1 14.7 %collective-permute-start.26 = (f32[1,2,48,128]{3,1,2,0:T(2,128)S(1)}, f32[1,2,48,128]{3,1,2,0:T(2,128)S(1)}, u32[]{:S(2)}, u32[]{:S(2)}) collective-permute-start(f32[1,2,48,128]{3,1,2,0:T(2,128)S(1)} %bitcast.240), channel_id=1, source_target_pairs={{256,0},{288,32},{320,64},{352,96},{384,128},{416,160},{448,192},{... | collective-permute-start | bytes 147464 | tf_op jit(solution)/shard_map/ppermute | solution.py:12
  195.8 6.5 %collective-permute-start.28 = (f32[1,2,48,128]{3,1,2,0:T(2,128)S(1)}, f32[1,2,48,128]{3,1,2,0:T(2,128)S(1)}, u32[]{:S(2)}, u32[]{:S(2)}) collective-permute-start(f32[1,2,48,128]{3,1,2,0:T(2,128)S(1)} %convolution_bitcast_fusion.1), channel_id=1, source_target_pairs={{32,0},{64,32},{96,64},{128,96},{160,128},{192,160},{224,192},{256... | collective-permute-start | bytes 147464 | tf_op jit(solution)/shard_map/ppermute | solution.py:12
  197.1 6.3 %collective-permute-start.27 = (f32[1,2,48,128]{3,1,2,0:T(2,128)S(1)}, f32[1,2,48,128]{3,1,2,0:T(2,128)S(1)}, u32[]{:S(2)}, u32[]{:S(2)}) collective-permute-start(f32[1,2,48,128]{3,1,2,0:T(2,128)S(1)} %convolution_bitcast_fusion.1), channel_id=1, source_target_pairs={{0,32},{32,64},{64,96},{96,128},{128,160},{160,192},{192,224},{224... | collective-permute-start | bytes 147464 | tf_op jit(solution)/shard_map/ppermute | solution.py:12
where the time goes:
time: 209 us; the launch traced here: 205 us
  starting transfers between devices  101 us (48%)
  waiting for transfers between devices  40.9 us (20%)
  between operations  21.3 us (10%)
  other arithmetic  19.2 us (9%)
  local copies, waits for them, and re-layouts  12.3 us (6%)
  matrix products  10.3 us (5%)
    ppermute x25, starting transfers between devices, passed_along(): lax.ppermute(value, axis, [(source, source + steps) for source in range(f...  93.8 us
    ppermute x25, waiting for transfers between devices, passed_along(): lax.ppermute(value, axis, [(source, source + steps) for source in range(f...  38.5 us
    dot_general x12, matrix products, mat_vec(): jnp.einsum('nij,njab->niab', left, vec, precision=lax.Precision.HIGHEST)  5.03 us
    ppermute x2, starting transfers between devices, with_halo(): lax.ppermute(lax.slice_in_dim(block, 0, width, axis=dim), axis, backward)  4.8 us
  transfers between devices with their start and end apart: 29, of which 11 were waited for; matrix products, arithmetic and copies ran while one was open for 12% of the time, Pallas kernels for 0%

commit v1 on v0

v1 whole, which is shorter than its diff:
```python
import functools

import jax
import jax.numpy as jnp
from jax import lax
from jax.experimental import pallas as pl
from jax.experimental.pallas import tpu as pltpu
from jax.sharding import PartitionSpec as P

MESH = pl.DeviceIdType.MESH
ANY = pl.BlockSpec(memory_space=pl.ANY)
VMEM = pl.BlockSpec(memory_space=pltpu.VMEM)
LANES = 128
WEIGHTS = (45.0, -9.0, 1.0)
SCALE = 0.2 / 60.0
NEAR = 4


def neighbour(axis, count, offset):
    return {axis: lax.rem(lax.axis_index(axis) + (offset + count), count)}


def stencil_matrix():
    source = lax.broadcasted_iota(jnp.int32, (2 * LANES, LANES), 0)
    target = lax.broadcasted_iota(jnp.int32, (2 * LANES, LANES), 1)
    own = source < LANES
    offset = jnp.where(own, source, source - LANES) - target
    matrix = jnp.zeros((2 * LANES, LANES), jnp.float32)
    for step, weight in enumerate(WEIGHTS, 1):
        for sign in (1, -1):
            inner = own & (offset == sign * step)
            wrapped = (source >= LANES) & (offset == sign * (step - LANES))
            matrix = jnp.where(inner | wrapped, sign * weight, matrix)
    return matrix.astype(jnp.bfloat16)


def along_z(own, halo, matrix):
    both = jnp.concatenate([own, halo], axis=1)
    high = both.astype(jnp.bfloat16)
    rest = both - high.astype(jnp.float32)
    middle = rest.astype(jnp.bfloat16)
    low = (rest - middle.astype(jnp.float32)).astype(jnp.bfloat16)
    dot = functools.partial(jnp.dot, preferred_element_type=jnp.float32)
    return dot(high, matrix) + (dot(middle, matrix) + dot(low, matrix))


def along_y(rows_at):
    total = None
    for step, weight in enumerate(WEIGHTS, 1):
        term = weight * (rows_at(step) - rows_at(-step))
        total = term if total is None else total + term
    return total


def pack_lanes(tiles):
    slot = lax.broadcasted_iota(jnp.int32, (8, LANES), 1) // 6
    packed = jnp.zeros((8, LANES), jnp.float32)
    for k, tile in enumerate(tiles):
        packed = jnp.where(slot == k, pltpu.roll(tile, 6 * k + 3, 1), packed)
    return packed


def unpack_lanes(from_left, from_right, count):
    lane = lax.broadcasted_iota(jnp.int32, (8, LANES), 1)
    both = jnp.where(lax.rem(lane, 6) < 3, from_left, from_right)
    return [pltpu.roll(both, (125 - 6 * k) % LANES, 1) for k in range(count)]


def tiles_of(planes):
    return [plane[8 * h : 8 * h + 8] for plane in planes for h in range(2)]


def solve_kernel(
    counts,
    density,
    momentum,
    face,
    local_out,
    phi_out,
    ends_out,
    face_s,
    state,
    flux_y,
    flux_zz,
    reduced_y,
    z_pack,
    z_left,
    z_right,
    send_a,
    recv_a,
    send_b,
    recv_b,
    coef,
    matrix_s,
    local,
    phi,
    in_sem,
    halo_send,
    halo_recv,
    a_send,
    a_recv,
    b_send,
    b_recv,
    out_sem,
    far_sem,
):
    nx, ny, nz = counts
    cells = state.shape[1]
    me = lax.axis_index("gx")

    barrier = pltpu.get_barrier_semaphore()
    near = [("gx", nx, k) for step in range(1, NEAR + 1) for k in (step, -step)]
    near += [("gy", ny, 1), ("gy", ny, -1), ("gz", nz, 1), ("gz", nz, -1)]
    for axis, count, offset in near:
        pl.semaphore_signal(
            barrier, inc=1, device_id=neighbour(axis, count, offset), device_id_type=MESH
        )
    loads = [
        pltpu.make_async_copy(face, face_s, in_sem.at[0]),
        pltpu.make_async_copy(density, state.at[0], in_sem.at[1]),
        pltpu.make_async_copy(momentum.at[0], state.at[1], in_sem.at[2]),
        pltpu.make_async_copy(momentum.at[1], state.at[2], in_sem.at[3]),
    ]
    for load in loads:
        load.start()
    matrix_s[...] = stencil_matrix()
    zero_rows = jnp.zeros((16, LANES), jnp.float32)
    send_b[pl.ds(6, 16, stride=8), :] = zero_rows
    send_b[pl.ds(7, 16, stride=8), :] = zero_rows
    for load in loads:
        load.wait()

    def inverse_face(i):
        return 1.0 / jnp.full((8, LANES), face_s[i], jnp.float32)

    def reduce_step(i, carry):
        pairs, base = carry
        inv = inverse_face(i)
        inv_rows = jnp.concatenate([inv, inv], 0)
        base = [(u + g * inv, g) for u, g in base]
        phi[0, i] = base[0][0]
        phi[1, i] = base[1][0]
        base = [(u, g + u) for u, g in base]
        rho, m0, m1 = state[0, i], state[1, i], state[2, i]
        over = 1.0 / rho
        speed_y = m0 * over
        speed_z = m1 * over
        yy, yz, zz = m0 * speed_y, m1 * speed_y, m1 * speed_z
        flux_y[0, i, 8:24] = m0
        flux_y[1, i, 8:24] = yy
        flux_y[2, i, 8:24] = yz
        flux_zz[i] = zz
        out = []
        for (u, g), value in zip(pairs, (rho, m0, m1, yy, yz, zz)):
            u = u + g * inv_rows
            out.append((u, g + (u - value)))
        return out, base

    def reduce_steps(block, carry):
        for k in range(4):
            carry = reduce_step(4 * block + k, carry)
        return carry

    zero = jnp.zeros((16, LANES), jnp.float32)
    unit = jnp.ones((8, LANES), jnp.float32)
    pairs, base = lax.fori_loop(
        0,
        cells // 4,
        reduce_steps,
        ([(zero, zero)] * 6, [(unit, 0.0 * unit), (0.0 * unit, unit)]),
    )
    rho_r, m0_r, m1_r, yy_r, yz_r, zz_r = pairs
    plain = [value for pair in (rho_r, m0_r, m1_r) for value in pair]
    by_y = [value for pair in (m0_r, yy_r, yz_r) for value in pair]
    by_z = [value for pair in (m1_r, yz_r, zz_r) for value in pair]
    for k in range(6):
        reduced_y[k, 8:24] = by_y[k]
    z_pack[cells // 2] = pack_lanes(tiles_of(by_z))

    pl.semaphore_wait(barrier, len(near))

    def halo(which, source, target, axis, count, offset):
        return pltpu.make_async_remote_copy(
            source,
            target,
            halo_send.at[which],
            halo_recv.at[which],
            device_id=neighbour(axis, count, offset),
            device_id_type=MESH,
        )

    last = cells // 2
    near_halos = [
        halo(0, reduced_y.at[:, 16:24], reduced_y.at[:, 0:8], "gy", ny, 1),
        halo(1, reduced_y.at[:, 8:16], reduced_y.at[:, 24:32], "gy", ny, -1),
        halo(2, z_pack.at[last], z_left.at[last], "gz", nz, 1),
        halo(3, z_pack.at[last], z_right.at[last], "gz", nz, -1),
    ]
    for copy in near_halos:
        copy.start()
    for offset in (NEAR, -NEAR):
        pl.semaphore_signal(
            far_sem, inc=1, device_id=neighbour("gx", nx, offset), device_id_type=MESH
        )
    raw_y = [
        halo(4, flux_y.at[:, :, 16:24], flux_y.at[:, :, 0:8], "gy", ny, 1),
        halo(5, flux_y.at[:, :, 8:16], flux_y.at[:, :, 24:32], "gy", ny, -1),
    ]
    for copy in raw_y:
        copy.start()

    (u1, g1), (u2, g2) = base
    low_half = lax.broadcasted_iota(jnp.int32, (8, LANES), 1) < LANES // 2
    row6 = jnp.where(low_half, u1, u2)
    row7 = jnp.where(low_half, g1, inverse_face(cells - 1))
    for h in range(2):
        send_a[pl.ds(64 * h + 6, 8, stride=8), :] = row6
        send_a[pl.ds(64 * h + 7, 8, stride=8), :] = row7

    for copy in near_halos:
        copy.wait_recv()
    own_z = jnp.concatenate(by_z, 0)
    halo_z = jnp.concatenate(unpack_lanes(z_left[last], z_right[last], 12), 0)
    diff_z = along_z(own_z, halo_z, matrix_s[...])
    for f in range(3):
        for v in range(2):
            k = 2 * f + v
            diff_y = along_y(lambda step: reduced_y[k, pl.ds(8 + step, 16), :])
            value = plain[k] - SCALE * (diff_y + diff_z[16 * k : 16 * k + 16])
            for h in range(2):
                send_a[pl.ds(64 * h + 3 * v + f, 8, stride=8), :] = value[8 * h : 8 * h + 8]

    def rows(index):
        return pl.ds(pl.multiple_of(index * 8, 8), 8)

    order = [k for step in range(nx // 2, 0, -1) for k in sorted({step, nx - step})]

    def exchange(source, target, send, recv, k):
        other = lax.rem(me + k, nx)
        return pltpu.make_async_remote_copy(
            source.at[rows(other)],
            target.at[rows(me)],
            send.at[k],
            recv.at[k],
            device_id={"gx": other},
            device_id_type=MESH,
        )

    pl.semaphore_wait(far_sem, 2)
    phase_a = [exchange(send_a, recv_a, a_send, a_recv, k) for k in order]
    for copy in phase_a:
        copy.start()
    recv_a[rows(me), :] = send_a[rows(me), :]

    def pack_step(p, _):
        planes = []
        for q in range(2):
            i = 2 * p + q
            planes += [state[2, i], flux_y[2, i, 8:24], flux_zz[i]]
        z_pack[p] = pack_lanes(tiles_of(planes))
        return _

    lax.fori_loop(0, last, pack_step, 0)
    raw_z = [
        halo(6, z_pack.at[0:last], z_left.at[0:last], "gz", nz, 1),
        halo(7, z_pack.at[0:last], z_right.at[0:last], "gz", nz, -1),
    ]
    for copy in raw_z:
        copy.start()
    for copy in raw_y + raw_z:
        copy.wait_recv()

    def local_step(p, carry):
        planes = []
        for q in range(2):
            i = 2 * p + q
            planes += [state[2, i], flux_y[2, i, 8:24], flux_zz[i]]
        halos = unpack_lanes(z_left[p], z_right[p], 12)
        diff_z = along_z(jnp.concatenate(planes, 0), jnp.concatenate(halos, 0), matrix_s[...])
        for q in range(2):
            i = 2 * p + q
            inv = inverse_face(i)
            inv_rows = jnp.concatenate([inv, inv], 0)
            new = []
            for f, (u, g) in enumerate(carry):
                diff_y = along_y(lambda step: flux_y[f, i, pl.ds(8 + step, 16), :])
                at = 16 * (3 * q + f)
                value = state[f, i] - SCALE * (diff_y + diff_z[at : at + 16])
                u = u + g * inv_rows
                local[f, i] = u
                new.append((u, g + (u - value)))
            carry = new
        return carry

    lax.fori_loop(0, last, local_step, [(zero, zero)] * 3)
    stores = [
        pltpu.make_async_copy(local, local_out, out_sem.at[0]),
        pltpu.make_async_copy(phi, phi_out, out_sem.at[1]),
    ]
    for store in stores:
        store.start()

    for copy in phase_a:
        copy.wait_recv()

    low_rows = lax.broadcasted_iota(jnp.int32, (16, LANES), 1) < LANES // 2
    row6 = recv_a[pl.ds(6, 16, stride=8), :]
    row7 = recv_a[pl.ds(7, 16, stride=8), :]
    turn6 = pltpu.roll(row6, LANES // 2, 1)
    turn7 = pltpu.roll(row7, LANES // 2, 1)
    t_uu = jnp.where(low_rows, row6, turn6)
    t_ug = jnp.where(low_rows, turn6, row6)
    t_gu = jnp.where(low_rows, row7, turn7)
    coef[0] = t_uu
    coef[1] = t_ug
    coef[2] = t_gu
    coef[3] = (1.0 + t_ug * t_gu) / t_uu
    coef[4] = jnp.where(low_rows, turn7, row7)

    def at_row(which, j):
        return jnp.broadcast_to(coef[which, pl.ds(j, 1), :], (3, LANES))

    blocks = [[at_row(which, j) for which in range(4)] for j in range(nx)]
    one = jnp.ones((3, LANES), jnp.float32)
    from_left = [(0.0 * one, one)]
    for j in range(nx):
        uu, ug, gu, gg = blocks[j]
        u, g = from_left[-1]
        from_left.append((uu * u + ug * g, gu * u + gg * g))
    from_right = [None] * nx + [(at_row(4, nx - 1), one)]
    for j in range(nx - 1, -1, -1):
        uu, ug, gu, gg = blocks[j]
        u, h = from_right[j + 1]
        from_right[j] = (gg * u + ug * h, gu * u + uu * h)
    norm = -1.0 / from_right[0][0]
    left_sums, right_terms = [0.0 * one], []
    for j in range(nx):
        u_r = recv_a[pl.ds(8 * j, 3), :]
        g_r = recv_a[pl.ds(8 * j + 3, 3), :]
        u, g = from_left[j + 1]
        left_sums.append(left_sums[-1] + (u * g_r - g * u_r))
        u, h = from_right[j + 1]
        right_terms.append(u * g_r + h * u_r)
    right_sum = 0.0 * one
    for d in range(nx - 1, -1, -1):
        right_sum = right_sum + right_terms[d]
        right, left = right_sum * norm, left_sums[d] * norm
        send_b[pl.ds(8 * d, 3), :] = right * from_left[d][0] + left * from_right[d][0]
        send_b[pl.ds(8 * d + 3, 3), :] = right * from_left[d][1] - left * from_right[d][1]

    phase_b = [exchange(send_b, recv_b, b_send, b_recv, k) for k in order]
    for copy in phase_b:
        copy.start()
    recv_b[rows(me), :] = send_b[rows(me), :]
    for copy in near_halos + raw_y + raw_z + phase_a:
        copy.wait_send()
    for store in stores:
        store.wait()
    for copy in phase_b:
        copy.wait_recv()
    for v in range(2):
        for f in range(3):
            ends_out[v, f] = recv_b[pl.ds(3 * v + f, 16, stride=8), :]
    for copy in phase_b:
        copy.wait_send()


def combine_kernel(local, phi, ends, out):
    starts = [(ends[0, f], ends[1, f]) for f in range(3)]
    for i in range(local.shape[1]):
        by_u = jnp.concatenate([phi[0, i]] * 2, 0)
        by_g = jnp.concatenate([phi[1, i]] * 2, 0)
        for f, (u, g) in enumerate(starts):
            out[f, i] = local[f, i] + (by_u * u + by_g * g)


def on_device(density, momentum, lower_face):
    counts = tuple(lax.axis_size(axis) for axis in ("gx", "gy", "gz"))
    nx = counts[0]
    cells, rows, lanes = density.shape
    block = (3, cells, rows, lanes)
    f32 = jnp.float32
    sems = pltpu.SemaphoreType.DMA
    local, phi, ends = pl.pallas_call(
        functools.partial(solve_kernel, counts),
        out_shape=(
            jax.ShapeDtypeStruct(block, f32),
            jax.ShapeDtypeStruct((2, cells, 8, lanes), f32),
            jax.ShapeDtypeStruct((2, 3, rows, lanes), f32),
        ),
        in_specs=[ANY, ANY, ANY],
        out_specs=(ANY, ANY, VMEM),
        scratch_shapes=[
            pltpu.SMEM((cells,), f32),
            pltpu.VMEM(block, f32),
            pltpu.VMEM((3, cells, 32, lanes), f32),
            pltpu.VMEM((cells, rows, lanes), f32),
            pltpu.VMEM((6, 32, lanes), f32),
            pltpu.VMEM((cells // 2 + 1, 8, lanes), f32),
            pltpu.VMEM((cells // 2 + 1, 8, lanes), f32),
            pltpu.VMEM((cells // 2 + 1, 8, lanes), f32),
            pltpu.VMEM((nx * 8, lanes), f32),
            pltpu.VMEM((nx * 8, lanes), f32),
            pltpu.VMEM((nx * 8, lanes), f32),
            pltpu.VMEM((nx * 8, lanes), f32),
            pltpu.VMEM((5, nx, lanes), f32),
            pltpu.VMEM((2 * lanes, lanes), jnp.bfloat16),
            pltpu.VMEM(block, f32),
            pltpu.VMEM((2, cells, 8, lanes), f32),
            sems((4,)),
            sems((8,)),
            sems((8,)),
            sems((nx,)),
            sems((nx,)),
            sems((nx,)),
            sems((nx,)),
            sems((2,)),
            pltpu.SemaphoreType.REGULAR,
        ],
        compiler_params=pltpu.CompilerParams(collective_id=0, has_side_effects=True),
        name="solve",
    )(density, momentum, lower_face)
    return pl.pallas_call(
        combine_kernel,
        out_shape=jax.ShapeDtypeStruct(block, f32),
        in_specs=[VMEM, VMEM, VMEM],
        out_specs=VMEM,
        name="combine",
    )(local, phi, ends)


def solution(mesh):
    placed = (P("gx", "gy", "gz"), P(None, "gx", "gy", "gz"), P("gx"))
    return jax.shard_map(
        on_device, mesh=mesh, in_specs=placed, out_specs=P(None, "gx", "gy", "gz"), check_vma=False
    )
```

time: 209 us -> 39 us (0.19); the launches traced: 205 us -> 38.8 us
  starting transfers between devices: 101 us -> 0 us
  waiting for transfers between devices: 40.9 us -> 0 us
  Pallas kernels: 0 us -> 38.8 us
  between operations: 21.3 us -> 0.01 us
  other arithmetic: 19.2 us -> 0 us
  local copies, waits for them, and re-layouts: 12.3 us -> 0 us
  matrix products: 10.3 us -> 0 us
    ppermute x29 -> x0, starting transfers between devices: 101 us -> none  [the longest x25 93.8 us: passed_along(): lax.ppermute(value, axis, [(source, source + steps) for source in range(f...]
    ppermute x29 -> x0, waiting for transfers between devices: 40.9 us -> none  [the longest x25 38.5 us: passed_along(): lax.ppermute(value, axis, [(source, source + steps) for source in range(f...]
    pallas_call x0 -> x2, Pallas kernels: none -> 38.8 us  [the longest x1 36.6 us: on_device(): pl.pallas_call(functools.partial(solve_kernel, counts), out_shape=(jax.Sh...]
    dot_general x33 -> x0, matrix products: 9.86 us -> none  [the longest x12 5.03 us: mat_vec(): jnp.einsum('nij,njab->niab', left, vec, precision=lax.Precision.HIGHEST)]
    another operation x8 -> x0, other arithmetic: 6.88 us -> none  [the longest x3 3.59 us: on_device(): factor = jnp.linalg.cholesky(block)]
    slice x13 -> x0, local copies, waits for them, and re-layouts: 6.71 us -> none  [the longest x4 2.63 us: invert_pair(): first = jnp.stack([mat[:, 1, 1], -mat[:, 0, 1]], -1)]
    div x4 -> x0, other arithmetic: 4.18 us -> none  [the longest x3 4.1 us: invert_pair(): return jnp.stack([first, second], 1) / det[:, None, None]]
    concatenate x3 -> x0, other arithmetic: 4.12 us -> none  [the longest x2 2.94 us: with_halo(): block = jnp.concatenate([low, block, high], axis=dim)]
  transfers between devices with their start and end apart: 29 -> 0, of which waited for: 11 -> 0; matrix products, arithmetic and copies ran while one was open for 12% -> 0% of each run, Pallas kernels for 0% -> 0%
where the time goes in v1:
time: 39 us; the launch traced here: 38.8 us
  Pallas kernels  38.8 us (99%)
    pallas_call x1, Pallas kernels, on_device(): pl.pallas_call(functools.partial(solve_kernel, counts), out_shape=(jax.Sh...  36.6 us
    pallas_call x1, Pallas kernels, on_device(): pl.pallas_call(combine_kernel, out_shape=jax.ShapeDtypeStruct(block, f32)...  2.21 us

profile of v1, /device:TPU:24, one launch (start us, length us, event | category | flops | bytes accessed | tf_op | source)
XLA Modules:
  0.0 38.8 jit_solution(52343118011613154)
XLA Ops:
  0.0 36.6 %solve.1 = (f32[3,32,16,128]{3,2,1,0:T(8,128)}, f32[2,32,8,128]{3,2,1,0:T(8,128)}, f32[2,3,16,128]{3,2,1,0:T(8,128)}) custom-call(f32[32,16,128]{2,1,0:T(8,128)} %density.1, f32[2,32,16,128]{3,2,1,0:T(8,128)} %momentum.1, f32[32]{0:T(128)} %face.1), custom_call_target="tpu_custom_call" | custom-call | tf_op jit(solution)/shard_map/solve/pallas_call | solution.py:384
  36.6 2.2 %combine.1 = f32[3,32,16,128]{3,2,1,0:T(8,128)} custom-call(f32[3,32,16,128]{3,2,1,0:T(8,128)} %get-tuple-element.8.local, f32[2,32,8,128]{3,2,1,0:T(8,128)} %get-tuple-element.9.phi, f32[2,3,16,128]{3,2,1,0:T(8,128)} %get-tuple-element.10.ends), custom_call_target="tpu_custom_call" | custom-call | tf_op jit(solution)/shard_map/combine/pallas_call | solution.py:423

commit v2 on v1

--- a/solution.py
+++ b/solution.py
@@ -10,6 +10,7 @@
 MESH = pl.DeviceIdType.MESH
 ANY = pl.BlockSpec(memory_space=pl.ANY)
 VMEM = pl.BlockSpec(memory_space=pltpu.VMEM)
+HBM = pl.BlockSpec(memory_space=pltpu.HBM)
 LANES = 128
 WEIGHTS = (45.0, -9.0, 1.0)
 SCALE = 0.2 / 60.0
@@ -124,9 +125,6 @@
     for load in loads:
         load.start()
     matrix_s[...] = stencil_matrix()
-    zero_rows = jnp.zeros((16, LANES), jnp.float32)
-    send_b[pl.ds(6, 16, stride=8), :] = zero_rows
-    send_b[pl.ds(7, 16, stride=8), :] = zero_rows
     for load in loads:
         load.wait()
 
@@ -191,8 +189,8 @@
 
     last = cells // 2
     near_halos = [
-        halo(0, reduced_y.at[:, 16:24], reduced_y.at[:, 0:8], "gy", ny, 1),
-        halo(1, reduced_y.at[:, 8:16], reduced_y.at[:, 24:32], "gy", ny, -1),
+        halo(0, reduced_y.at[:, 21:24], reduced_y.at[:, 5:8], "gy", ny, 1),
+        halo(1, reduced_y.at[:, 8:11], reduced_y.at[:, 24:27], "gy", ny, -1),
         halo(2, z_pack.at[last], z_left.at[last], "gz", nz, 1),
         halo(3, z_pack.at[last], z_right.at[last], "gz", nz, -1),
     ]
@@ -203,19 +201,37 @@
             far_sem, inc=1, device_id=neighbour("gx", nx, offset), device_id_type=MESH
         )
     raw_y = [
-        halo(4, flux_y.at[:, :, 16:24], flux_y.at[:, :, 0:8], "gy", ny, 1),
-        halo(5, flux_y.at[:, :, 8:16], flux_y.at[:, :, 24:32], "gy", ny, -1),
+        halo(4, flux_y.at[:, :, 21:24], flux_y.at[:, :, 5:8], "gy", ny, 1),
+        halo(5, flux_y.at[:, :, 8:11], flux_y.at[:, :, 24:27], "gy", ny, -1),
     ]
     for copy in raw_y:
         copy.start()
 
     (u1, g1), (u2, g2) = base
-    low_half = lax.broadcasted_iota(jnp.int32, (8, LANES), 1) < LANES // 2
-    row6 = jnp.where(low_half, u1, u2)
-    row7 = jnp.where(low_half, g1, inverse_face(cells - 1))
+    quarter = lax.broadcasted_iota(jnp.int32, (8, LANES), 1) // 32
+    row6 = jnp.where(
+        quarter < 2,
+        jnp.where(quarter == 0, u1, u2),
+        jnp.where(quarter == 2, g1, inverse_face(cells - 1)),
+    )
     for h in range(2):
         send_a[pl.ds(64 * h + 6, 8, stride=8), :] = row6
-        send_a[pl.ds(64 * h + 7, 8, stride=8), :] = row7
+
+    def pack_step(p, _):
+        planes = []
+        for q in range(2):
+            i = 2 * p + q
+            planes += [state[2, i], flux_y[2, i, 8:24], flux_zz[i]]
+        z_pack[p] = pack_lanes(tiles_of(planes))
+        return _
+
+    lax.fori_loop(0, last, pack_step, 0)
+    raw_z = [
+        halo(6, z_pack.at[0:last], z_left.at[0:last], "gz", nz, 1),
+        halo(7, z_pack.at[0:last], z_right.at[0:last], "gz", nz, -1),
+    ]
+    for copy in raw_z:
+        copy.start()
 
     for copy in near_halos:
         copy.wait_recv()
@@ -230,16 +246,16 @@
             for h in range(2):
                 send_a[pl.ds(64 * h + 3 * v + f, 8, stride=8), :] = value[8 * h : 8 * h + 8]
 
-    def rows(index):
-        return pl.ds(pl.multiple_of(index * 8, 8), 8)
-
     order = [k for step in range(nx // 2, 0, -1) for k in sorted({step, nx - step})]
 
-    def exchange(source, target, send, recv, k):
+    def rows(index, count):
+        return pl.ds(pl.multiple_of(index * 8, 8), count)
+
+    def exchange(source, target, count, send, recv, k):
         other = lax.rem(me + k, nx)
         return pltpu.make_async_remote_copy(
-            source.at[rows(other)],
-            target.at[rows(me)],
+            source.at[rows(other, count)],
+            target.at[rows(me, count)],
             send.at[k],
             recv.at[k],
             device_id={"gx": other},
@@ -247,75 +263,33 @@
         )
 
     pl.semaphore_wait(far_sem, 2)
-    phase_a = [exchange(send_a, recv_a, a_send, a_recv, k) for k in order]
+    phase_a = [exchange(send_a, recv_a, 7, a_send, a_recv, k) for k in order]
     for copy in phase_a:
         copy.start()
-    recv_a[rows(me), :] = send_a[rows(me), :]
-
-    def pack_step(p, _):
-        planes = []
-        for q in range(2):
-            i = 2 * p + q
-            planes += [state[2, i], flux_y[2, i, 8:24], flux_zz[i]]
-        z_pack[p] = pack_lanes(tiles_of(planes))
-        return _
-
-    lax.fori_loop(0, last, pack_step, 0)
-    raw_z = [
-        halo(6, z_pack.at[0:last], z_left.at[0:last], "gz", nz, 1),
-        halo(7, z_pack.at[0:last], z_right.at[0:last], "gz", nz, -1),
-    ]
-    for copy in raw_z:
-        copy.start()
-    for copy in raw_y + raw_z:
-        copy.wait_recv()
-
-    def local_step(p, carry):
-        planes = []
-        for q in range(2):
-            i = 2 * p + q
-            planes += [state[2, i], flux_y[2, i, 8:24], flux_zz[i]]
-        halos = unpack_lanes(z_left[p], z_right[p], 12)
-        diff_z = along_z(jnp.concatenate(planes, 0), jnp.concatenate(halos, 0), matrix_s[...])
-        for q in range(2):
-            i = 2 * p + q
-            inv = inverse_face(i)
-            inv_rows = jnp.concatenate([inv, inv], 0)
-            new = []
-            for f, (u, g) in enumerate(carry):
-                diff_y = along_y(lambda step: flux_y[f, i, pl.ds(8 + step, 16), :])
-                at = 16 * (3 * q + f)
-                value = state[f, i] - SCALE * (diff_y + diff_z[at : at + 16])
-                u = u + g * inv_rows
-                local[f, i] = u
-                new.append((u, g + (u - value)))
-            carry = new
-        return carry
-
-    lax.fori_loop(0, last, local_step, [(zero, zero)] * 3)
-    stores = [
-        pltpu.make_async_copy(local, local_out, out_sem.at[0]),
-        pltpu.make_async_copy(phi, phi_out, out_sem.at[1]),
-    ]
-    for store in stores:
-        store.start()
+    recv_a[rows(me, 7), :] = send_a[rows(me, 7), :]
 
     for copy in phase_a:
         copy.wait_recv()
 
-    low_rows = lax.broadcasted_iota(jnp.int32, (16, LANES), 1) < LANES // 2
+    quarter = lax.broadcasted_iota(jnp.int32, (16, LANES), 1) // 32
     row6 = recv_a[pl.ds(6, 16, stride=8), :]
-    row7 = recv_a[pl.ds(7, 16, stride=8), :]
-    turn6 = pltpu.roll(row6, LANES // 2, 1)
-    turn7 = pltpu.roll(row7, LANES // 2, 1)
-    t_uu = jnp.where(low_rows, row6, turn6)
-    t_ug = jnp.where(low_rows, turn6, row6)
-    t_gu = jnp.where(low_rows, row7, turn7)
+    turns = [row6] + [pltpu.roll(row6, 32 * k, 1) for k in (1, 2, 3)]
+
+    def spread(which):
+        odd = (quarter - which) & 1
+        high = (quarter - which) & 2
+        return jnp.where(
+            high == 0,
+            jnp.where(odd == 0, turns[0], turns[1]),
+            jnp.where(odd == 0, turns[2], turns[3]),
+        )
+
+    t_uu, t_ug, t_gu = spread(0), spread(1), spread(2)
     coef[0] = t_uu
     coef[1] = t_ug
     coef[2] = t_gu
     coef[3] = (1.0 + t_ug * t_gu) / t_uu
-    coef[4] = jnp.where(low_rows, turn7, row7)
+    coef[4] = spread(3)
 
     def at_row(which, j):
         return jnp.broadcast_to(coef[which, pl.ds(j, 1), :], (3, LANES))
@@ -348,10 +322,43 @@
         send_b[pl.ds(8 * d, 3), :] = right * from_left[d][0] + left * from_right[d][0]
         send_b[pl.ds(8 * d + 3, 3), :] = right * from_left[d][1] - left * from_right[d][1]
 
-    phase_b = [exchange(send_b, recv_b, b_send, b_recv, k) for k in order]
+    phase_b = [exchange(send_b, recv_b, 6, b_send, b_recv, k) for k in order]
     for copy in phase_b:
         copy.start()
-    recv_b[rows(me), :] = send_b[rows(me), :]
+    recv_b[rows(me, 6), :] = send_b[rows(me, 6), :]
+
+    for copy in raw_y + raw_z:
+        copy.wait_recv()
+
+    def local_step(p, carry):
+        planes = []
+        for q in range(2):
+            i = 2 * p + q
+            planes += [state[2, i], flux_y[2, i, 8:24], flux_zz[i]]
+        halos = unpack_lanes(z_left[p], z_right[p], 12)
+        diff_z = along_z(jnp.concatenate(planes, 0), jnp.concatenate(halos, 0), matrix_s[...])
+        for q in range(2):
+            i = 2 * p + q
+            inv = inverse_face(i)
+            inv_rows = jnp.concatenate([inv, inv], 0)
+            new = []
+            for f, (u, g) in enumerate(carry):
+                diff_y = along_y(lambda step: flux_y[f, i, pl.ds(8 + step, 16), :])
+                at = 16 * (3 * q + f)
+                value = state[f, i] - SCALE * (diff_y + diff_z[at : at + 16])
+                u = u + g * inv_rows
+                local[f, i] = u
+                new.append((u, g + (u - value)))
+            carry = new
+        return carry
+
+    lax.fori_loop(0, last, local_step, [(zero, zero)] * 3)
+    stores = [
+        pltpu.make_async_copy(local, local_out, out_sem.at[0]),
+        pltpu.make_async_copy(phi, phi_out, out_sem.at[1]),
+    ]
+    for store in stores:
+        store.start()
     for copy in near_halos + raw_y + raw_z + phase_a:
         copy.wait_send()
     for store in stores:
@@ -388,7 +395,7 @@
             jax.ShapeDtypeStruct((2, cells, 8, lanes), f32),
             jax.ShapeDtypeStruct((2, 3, rows, lanes), f32),
         ),
-        in_specs=[ANY, ANY, ANY],
+        in_specs=[HBM, HBM, HBM],
         out_specs=(ANY, ANY, VMEM),
         scratch_shapes=[
             pltpu.SMEM((cells,), f32),
@@ -417,14 +424,17 @@
             sems((2,)),
             pltpu.SemaphoreType.REGULAR,
         ],
-        compiler_params=pltpu.CompilerParams(collective_id=0, has_side_effects=True),
+        compiler_params=pltpu.CompilerParams(
+            collective_id=0, has_side_effects=True, vmem_limit_bytes=16 << 20
+        ),
         name="solve",
-    )(density, momentum, lower_face)
+    )(*(pltpu.with_memory_space_constraint(x, pltpu.HBM) for x in (density, momentum, lower_face)))
     return pl.pallas_call(
         combine_kernel,
         out_shape=jax.ShapeDtypeStruct(block, f32),
         in_specs=[VMEM, VMEM, VMEM],
         out_specs=VMEM,
+        compiler_params=pltpu.CompilerParams(vmem_limit_bytes=16 << 20),
         name="combine",
     )(local, phi, ends)
 

time: 39 us -> 32.6 us (0.84)
  Pallas kernels: 38.8 us -> 32.5 us
    pallas_call x1, Pallas kernels: 36.6 us -> 31.5 us  [on_device(): pl.pallas_call(functools.partial(solve_kernel, counts), out_shape=(jax.Sh...]
    pallas_call x1, Pallas kernels: 2.21 us -> 0.99 us  [on_device(): pl.pallas_call(combine_kernel, out_shape=jax.ShapeDtypeStruct(block, f32)...]
where the time goes in v2:
time: 32.6 us; the launch traced here: 32.5 us
  Pallas kernels  32.5 us (100%)
    pallas_call x1, Pallas kernels, on_device(): pl.pallas_call(functools.partial(solve_kernel, counts), out_shape=(jax.Sh...  31.5 us
    pallas_call x1, Pallas kernels, on_device(): pl.pallas_call(combine_kernel, out_shape=jax.ShapeDtypeStruct(block, f32)...  0.99 us

profile of v2, /device:TPU:24, one launch (start us, length us, event | category | flops | bytes accessed | tf_op | source)
XLA Modules:
  0.0 32.5 jit_solution(15078683446313098444)
XLA Ops:
  0.0 31.5 %solve.1 = (f32[3,32,16,128]{3,2,1,0:T(8,128)S(1)}, f32[2,32,8,128]{3,2,1,0:T(8,128)S(1)}, f32[2,3,16,128]{3,2,1,0:T(8,128)S(1)}) custom-call(f32[32,16,128]{2,1,0:T(8,128)} %density.1, f32[2,32,16,128]{3,2,1,0:T(8,128)} %momentum.1, f32[32]{0:T(128)} %face.1), custom_call_target="tpu_custom_call" | custom-call | tf_op jit(solution)/shard_map/solve/pallas_call | solution.py:391
  31.5 1.0 %combine.1 = f32[3,32,16,128]{3,2,1,0:T(8,128)} custom-call(f32[3,32,16,128]{3,2,1,0:T(8,128)S(1)} %get-tuple-element.8.local, f32[2,32,8,128]{3,2,1,0:T(8,128)S(1)} %get-tuple-element.9.phi, f32[2,3,16,128]{3,2,1,0:T(8,128)S(1)} %get-tuple-element.10.ends), custom_call_target="tpu_custom_call" | custom-call | tf_op jit(solution)/shard_map/combine/pallas_call | solution.py:432

commit v3 on v2

--- a/solution.py
+++ b/solution.py
@@ -15,6 +15,12 @@
 WEIGHTS = (45.0, -9.0, 1.0)
 SCALE = 0.2 / 60.0
 NEAR = 4
+OWNER_LIST = (11, 12, 14, 15, 0, 1, 3, 4)
+OWNERS = 8
+EACH = 2
+SLOT = 16
+A_ORDER = (0, 7, 1, 6, 2, 5, 3, 4)
+B_ORDER = (0, 1, 2, 3, 4, 5, 6, 7, 15, 14, 13, 12, 8, 9, 10, 11)
 
 
 def neighbour(axis, count, offset):
@@ -69,6 +75,68 @@
 
 def tiles_of(planes):
     return [plane[8 * h : 8 * h + 8] for plane in planes for h in range(2)]
+
+
+def own_rows(nx, mine, recv_a, send_b, recv_b, coef, to_owner, to_block, rows):
+    me = lax.axis_index("gx")
+    for j in range(nx):
+        pl.when(me != j)(to_owner(0, j).wait_recv)
+    quarter = lax.broadcasted_iota(jnp.int32, (nx, LANES), 1) // 32
+    row6 = recv_a[pl.ds(6 * EACH, nx, stride=SLOT), :]
+    turns = [row6] + [pltpu.roll(row6, 32 * k, 1) for k in (1, 2, 3)]
+
+    def spread(which):
+        odd = (quarter - which) & 1
+        high = (quarter - which) & 2
+        return jnp.where(
+            high == 0,
+            jnp.where(odd == 0, turns[0], turns[1]),
+            jnp.where(odd == 0, turns[2], turns[3]),
+        )
+
+    t_uu, t_ug, t_gu = spread(0), spread(1), spread(2)
+    coef[0] = t_uu
+    coef[1] = t_ug
+    coef[2] = t_gu
+    coef[3] = (1.0 + t_ug * t_gu) / t_uu
+    coef[4] = spread(3)
+
+    def at_row(which, j):
+        return jnp.broadcast_to(coef[which, pl.ds(j, 1), :], (3 * EACH, LANES))
+
+    blocks = [[at_row(which, j) for which in range(4)] for j in range(nx)]
+    one = jnp.ones((3 * EACH, LANES), jnp.float32)
+    from_left = [(0.0 * one, one)]
+    for j in range(nx):
+        uu, ug, gu, gg = blocks[j]
+        u, g = from_left[-1]
+        from_left.append((uu * u + ug * g, gu * u + gg * g))
+    from_right = [None] * nx + [(at_row(4, nx - 1), one)]
+    for j in range(nx - 1, -1, -1):
+        uu, ug, gu, gg = blocks[j]
+        u, h = from_right[j + 1]
+        from_right[j] = (gg * u + ug * h, gu * u + uu * h)
+    norm = -1.0 / from_right[0][0]
+    left_sums, right_terms = [0.0 * one], []
+    for j in range(nx):
+        u_r = recv_a[pl.ds(SLOT * j, 3 * EACH), :]
+        g_r = recv_a[pl.ds(SLOT * j + 3 * EACH, 3 * EACH), :]
+        u, g = from_left[j + 1]
+        left_sums.append(left_sums[-1] + (u * g_r - g * u_r))
+        u, h = from_right[j + 1]
+        right_terms.append(u * g_r + h * u_r)
+    right_sum = 0.0 * one
+    for d in range(nx - 1, -1, -1):
+        right_sum = right_sum + right_terms[d]
+        right, left = right_sum * norm, left_sums[d] * norm
+        send_b[pl.ds(SLOT * d, 3 * EACH), :] = right * from_left[d][0] + left * from_right[d][0]
+        send_b[pl.ds(SLOT * d + 3 * EACH, 3 * EACH), :] = right * from_left[d][1] - left * from_right[d][1]
+    for d in B_ORDER:
+        pl.when(me != d)(to_block(mine, d).start)
+
+        @pl.when(me == d)
+        def _():
+            recv_b[rows(mine, 6 * EACH), :] = send_b[rows(d, 6 * EACH), :]
 
 
 def solve_kernel(
@@ -110,7 +178,7 @@
     me = lax.axis_index("gx")
 
     barrier = pltpu.get_barrier_semaphore()
-    near = [("gx", nx, k) for step in range(1, NEAR + 1) for k in (step, -step)]
+    near = [("gx", nx, k) for step in range(NEAR, 0, -1) for k in (step, -step)]
     near += [("gy", ny, 1), ("gy", ny, -1), ("gz", nz, 1), ("gz", nz, -1)]
     for axis, count, offset in near:
         pl.semaphore_signal(
@@ -176,6 +244,10 @@
     z_pack[cells // 2] = pack_lanes(tiles_of(by_z))
 
     pl.semaphore_wait(barrier, len(near))
+    for offset in (NEAR, -NEAR):
+        pl.semaphore_signal(
+            far_sem, inc=1, device_id=neighbour("gx", nx, offset), device_id_type=MESH
+        )
 
     def halo(which, source, target, axis, count, offset):
         return pltpu.make_async_remote_copy(
@@ -196,10 +268,6 @@
     ]
     for copy in near_halos:
         copy.start()
-    for offset in (NEAR, -NEAR):
-        pl.semaphore_signal(
-            far_sem, inc=1, device_id=neighbour("gx", nx, offset), device_id_type=MESH
-        )
     raw_y = [
         halo(4, flux_y.at[:, :, 21:24], flux_y.at[:, :, 5:8], "gy", ny, 1),
         halo(5, flux_y.at[:, :, 8:11], flux_y.at[:, :, 24:27], "gy", ny, -1),
@@ -214,8 +282,7 @@
         jnp.where(quarter == 0, u1, u2),
         jnp.where(quarter == 2, g1, inverse_face(cells - 1)),
     )
-    for h in range(2):
-        send_a[pl.ds(64 * h + 6, 8, stride=8), :] = row6
+    send_a[pl.ds(6 * EACH, OWNERS, stride=SLOT), :] = jnp.concatenate([row6] * (OWNERS // 8), 0)
 
     def pack_step(p, _):
         planes = []
@@ -243,89 +310,45 @@
             k = 2 * f + v
             diff_y = along_y(lambda step: reduced_y[k, pl.ds(8 + step, 16), :])
             value = plain[k] - SCALE * (diff_y + diff_z[16 * k : 16 * k + 16])
-            for h in range(2):
-                send_a[pl.ds(64 * h + 3 * v + f, 8, stride=8), :] = value[8 * h : 8 * h + 8]
-
-    order = [k for step in range(nx // 2, 0, -1) for k in sorted({step, nx - step})]
+            for r in range(EACH):
+                at = EACH * (3 * v + f) + r
+                part = value[OWNERS * r : OWNERS * (r + 1)]
+                send_a[pl.ds(at, OWNERS, stride=SLOT), :] = part
 
     def rows(index, count):
-        return pl.ds(pl.multiple_of(index * 8, 8), count)
-
-    def exchange(source, target, count, send, recv, k):
-        other = lax.rem(me + k, nx)
+        return pl.ds(pl.multiple_of(index * SLOT, 8), count)
+
+    owners = OWNER_LIST
+    mine = sum(c * (me == owner).astype(jnp.int32) for c, owner in enumerate(owners))
+    is_owner = functools.reduce(jnp.logical_or, [me == owner for owner in owners])
+
+    def to_owner(c, source):
         return pltpu.make_async_remote_copy(
-            source.at[rows(other, count)],
-            target.at[rows(me, count)],
-            send.at[k],
-            recv.at[k],
-            device_id={"gx": other},
+            send_a.at[rows(c, 6 * EACH + 1)],
+            recv_a.at[rows(source, 6 * EACH + 1)],
+            a_send.at[c],
+            a_recv.at[source],
+            device_id={"gx": owners[c]},
             device_id_type=MESH,
         )
 
+    def to_block(c, target):
+        return pltpu.make_async_remote_copy(
+            send_b.at[rows(target, 6 * EACH)],
+            recv_b.at[rows(c, 6 * EACH)],
+            b_send.at[target],
+            b_recv.at[c],
+            device_id={"gx": target},
+            device_id_type=MESH,
+        )
+
     pl.semaphore_wait(far_sem, 2)
-    phase_a = [exchange(send_a, recv_a, 7, a_send, a_recv, k) for k in order]
-    for copy in phase_a:
-        copy.start()
-    recv_a[rows(me, 7), :] = send_a[rows(me, 7), :]
-
-    for copy in phase_a:
-        copy.wait_recv()
-
-    quarter = lax.broadcasted_iota(jnp.int32, (16, LANES), 1) // 32
-    row6 = recv_a[pl.ds(6, 16, stride=8), :]
-    turns = [row6] + [pltpu.roll(row6, 32 * k, 1) for k in (1, 2, 3)]
-
-    def spread(which):
-        odd = (quarter - which) & 1
-        high = (quarter - which) & 2
-        return jnp.where(
-            high == 0,
-            jnp.where(odd == 0, turns[0], turns[1]),
-            jnp.where(odd == 0, turns[2], turns[3]),
-        )
-
-    t_uu, t_ug, t_gu = spread(0), spread(1), spread(2)
-    coef[0] = t_uu
-    coef[1] = t_ug
-    coef[2] = t_gu
-    coef[3] = (1.0 + t_ug * t_gu) / t_uu
-    coef[4] = spread(3)
-
-    def at_row(which, j):
-        return jnp.broadcast_to(coef[which, pl.ds(j, 1), :], (3, LANES))
-
-    blocks = [[at_row(which, j) for which in range(4)] for j in range(nx)]
-    one = jnp.ones((3, LANES), jnp.float32)
-    from_left = [(0.0 * one, one)]
-    for j in range(nx):
-        uu, ug, gu, gg = blocks[j]
-        u, g = from_left[-1]
-        from_left.append((uu * u + ug * g, gu * u + gg * g))
-    from_right = [None] * nx + [(at_row(4, nx - 1), one)]
-    for j in range(nx - 1, -1, -1):
-        uu, ug, gu, gg = blocks[j]
-        u, h = from_right[j + 1]
-        from_right[j] = (gg * u + ug * h, gu * u + uu * h)
-    norm = -1.0 / from_right[0][0]
-    left_sums, right_terms = [0.0 * one], []
-    for j in range(nx):
-        u_r = recv_a[pl.ds(8 * j, 3), :]
-        g_r = recv_a[pl.ds(8 * j + 3, 3), :]
-        u, g = from_left[j + 1]
-        left_sums.append(left_sums[-1] + (u * g_r - g * u_r))
-        u, h = from_right[j + 1]
-        right_terms.append(u * g_r + h * u_r)
-    right_sum = 0.0 * one
-    for d in range(nx - 1, -1, -1):
-        right_sum = right_sum + right_terms[d]
-        right, left = right_sum * norm, left_sums[d] * norm
-        send_b[pl.ds(8 * d, 3), :] = right * from_left[d][0] + left * from_right[d][0]
-        send_b[pl.ds(8 * d + 3, 3), :] = right * from_left[d][1] - left * from_right[d][1]
-
-    phase_b = [exchange(send_b, recv_b, 6, b_send, b_recv, k) for k in order]
-    for copy in phase_b:
-        copy.start()
-    recv_b[rows(me, 6), :] = send_b[rows(me, 6), :]
+    for c in A_ORDER:
+        pl.when(me != owners[c])(to_owner(c, me).start)
+
+        @pl.when(me == owners[c])
+        def _():
+            recv_a[rows(me, 6 * EACH + 1), :] = send_a[rows(c, 6 * EACH + 1), :]
 
     for copy in raw_y + raw_z:
         copy.wait_recv()
@@ -359,17 +382,27 @@
     ]
     for store in stores:
         store.start()
-    for copy in near_halos + raw_y + raw_z + phase_a:
+
+    @pl.when(is_owner)
+    def _():
+        own_rows(nx, mine, recv_a, send_b, recv_b, coef, to_owner, to_block, rows)
+
+    for copy in near_halos + raw_y + raw_z:
         copy.wait_send()
     for store in stores:
         store.wait()
-    for copy in phase_b:
-        copy.wait_recv()
+    for c in range(OWNERS):
+        pl.when(me != owners[c])(to_block(c, me).wait_recv)
     for v in range(2):
         for f in range(3):
-            ends_out[v, f] = recv_b[pl.ds(3 * v + f, 16, stride=8), :]
-    for copy in phase_b:
-        copy.wait_send()
+            for r in range(EACH):
+                at = EACH * (3 * v + f) + r
+                part = recv_b[pl.ds(at, OWNERS, stride=SLOT), :]
+                ends_out[v, f, OWNERS * r : OWNERS * (r + 1)] = part
+    for c in range(OWNERS):
+        pl.when(me != owners[c])(to_owner(c, me).wait_send)
+    for d in range(nx):
+        pl.when(is_owner & (me != d))(to_block(mine, d).wait_send)
 
 
 def combine_kernel(local, phi, ends, out):
@@ -406,10 +439,10 @@
             pltpu.VMEM((cells // 2 + 1, 8, lanes), f32),
             pltpu.VMEM((cells // 2 + 1, 8, lanes), f32),
             pltpu.VMEM((cells // 2 + 1, 8, lanes), f32),
-            pltpu.VMEM((nx * 8, lanes), f32),
-            pltpu.VMEM((nx * 8, lanes), f32),
-            pltpu.VMEM((nx * 8, lanes), f32),
-            pltpu.VMEM((nx * 8, lanes), f32),
+            pltpu.VMEM((OWNERS * SLOT, lanes), f32),
+            pltpu.VMEM((nx * SLOT, lanes), f32),
+            pltpu.VMEM((nx * SLOT, lanes), f32),
+            pltpu.VMEM((OWNERS * SLOT, lanes), f32),
             pltpu.VMEM((5, nx, lanes), f32),
             pltpu.VMEM((2 * lanes, lanes), jnp.bfloat16),
             pltpu.VMEM(block, f32),

time: 32.6 us -> 31.3 us (0.960)
  Pallas kernels: 32.5 us -> 31 us
    pallas_call x1, Pallas kernels: 31.5 us -> 30 us  [on_device(): pl.pallas_call(functools.partial(solve_kernel, counts), out_shape=(jax.Sh...]
where the time goes in v3:
time: 31.3 us; the launch traced here: 31 us
  Pallas kernels  31 us (99%)
    pallas_call x1, Pallas kernels, on_device(): pl.pallas_call(functools.partial(solve_kernel, counts), out_shape=(jax.Sh...  30 us
    pallas_call x1, Pallas kernels, on_device(): pl.pallas_call(combine_kernel, out_shape=jax.ShapeDtypeStruct(block, f32)...  0.99 us

profile of v3, /device:TPU:24, one launch (start us, length us, event | category | flops | bytes accessed | tf_op | source)
XLA Modules:
  0.0 31.0 jit_solution(687172109715424119)
XLA Ops:
  0.0 30.0 %solve.1 = (f32[3,32,16,128]{3,2,1,0:T(8,128)S(1)}, f32[2,32,8,128]{3,2,1,0:T(8,128)S(1)}, f32[2,3,16,128]{3,2,1,0:T(8,128)S(1)}) custom-call(f32[32,16,128]{2,1,0:T(8,128)} %density.1, f32[2,32,16,128]{3,2,1,0:T(8,128)} %momentum.1, f32[32]{0:T(128)} %face.1), custom_call_target="tpu_custom_call" | custom-call | tf_op jit(solution)/shard_map/solve/pallas_call | solution.py:424
  30.1 1.0 %combine.1 = f32[3,32,16,128]{3,2,1,0:T(8,128)} custom-call(f32[3,32,16,128]{3,2,1,0:T(8,128)S(1)} %get-tuple-element.8.local, f32[2,32,8,128]{3,2,1,0:T(8,128)S(1)} %get-tuple-element.9.phi, f32[2,3,16,128]{3,2,1,0:T(8,128)S(1)} %get-tuple-element.10.ends), custom_call_target="tpu_custom_call" | custom-call | tf_op jit(solution)/shard_map/combine/pallas_call | solution.py:465

commit v4 on v3

--- a/solution.py
+++ b/solution.py
@@ -15,6 +15,7 @@
 WEIGHTS = (45.0, -9.0, 1.0)
 SCALE = 0.2 / 60.0
 NEAR = 4
+PARTS = 4
 OWNER_LIST = (11, 12, 14, 15, 0, 1, 3, 4)
 OWNERS = 8
 EACH = 2
@@ -405,13 +406,23 @@
         pl.when(is_owner & (me != d))(to_block(mine, d).wait_send)
 
 
-def combine_kernel(local, phi, ends, out):
+def combine_kernel(local, phi, ends, out, staged, sems):
     starts = [(ends[0, f], ends[1, f]) for f in range(3)]
-    for i in range(local.shape[1]):
-        by_u = jnp.concatenate([phi[0, i]] * 2, 0)
-        by_g = jnp.concatenate([phi[1, i]] * 2, 0)
-        for f, (u, g) in enumerate(starts):
-            out[f, i] = local[f, i] + (by_u * u + by_g * g)
+    cells = local.shape[1]
+    size = cells // PARTS
+    stores = []
+    for part in range(PARTS):
+        span = pl.ds(part * size, size)
+        for i in range(part * size, (part + 1) * size):
+            by_u = jnp.concatenate([phi[0, i]] * 2, 0)
+            by_g = jnp.concatenate([phi[1, i]] * 2, 0)
+            for f, (u, g) in enumerate(starts):
+                staged[f, i] = local[f, i] + (by_u * u + by_g * g)
+        store = pltpu.make_async_copy(staged.at[:, span], out.at[:, span], sems.at[part])
+        store.start()
+        stores.append(store)
+    for store in stores:
+        store.wait()
 
 
 def on_device(density, momentum, lower_face):
@@ -466,7 +477,8 @@
         combine_kernel,
         out_shape=jax.ShapeDtypeStruct(block, f32),
         in_specs=[VMEM, VMEM, VMEM],
-        out_specs=VMEM,
+        out_specs=ANY,
+        scratch_shapes=[pltpu.VMEM(block, f32), sems((PARTS,))],
         compiler_params=pltpu.CompilerParams(vmem_limit_bytes=16 << 20),
         name="combine",
     )(local, phi, ends)

time: 31.3 us -> 31.2 us (level)
  no operation moved by 1% of the time
where the time goes in v4:
time: 31.2 us; the launch traced here: 31 us
  Pallas kernels  31 us (99%)
    pallas_call x1, Pallas kernels, on_device(): pl.pallas_call(functools.partial(solve_kernel, counts), out_shape=(jax.Sh...  30 us
    pallas_call x1, Pallas kernels, on_device(): pl.pallas_call(combine_kernel, out_shape=jax.ShapeDtypeStruct(block, f32)...  0.94 us

profile of v4, /device:TPU:24, one launch (start us, length us, event | category | flops | bytes accessed | tf_op | source)
XLA Modules:
  0.0 31.0 jit_solution(18161935730761373724)
XLA Ops:
  0.0 30.0 %solve.1 = (f32[3,32,16,128]{3,2,1,0:T(8,128)S(1)}, f32[2,32,8,128]{3,2,1,0:T(8,128)S(1)}, f32[2,3,16,128]{3,2,1,0:T(8,128)S(1)}) custom-call(f32[32,16,128]{2,1,0:T(8,128)} %density.1, f32[2,32,16,128]{3,2,1,0:T(8,128)} %momentum.1, f32[32]{0:T(128)} %face.1), custom_call_target="tpu_custom_call" | custom-call | tf_op jit(solution)/shard_map/solve/pallas_call | solution.py:435
  30.1 0.9 %combine.1 = f32[3,32,16,128]{3,2,1,0:T(8,128)} custom-call(f32[3,32,16,128]{3,2,1,0:T(8,128)S(1)} %get-tuple-element.8.local, f32[2,32,8,128]{3,2,1,0:T(8,128)S(1)} %get-tuple-element.9.phi, f32[2,3,16,128]{3,2,1,0:T(8,128)S(1)} %get-tuple-element.10.ends), custom_call_target="tpu_custom_call" | custom-call | tf_op jit(solution)/shard_map/combine/pallas_call | solution.py:476

commit v5 on v4

--- a/solution.py
+++ b/solution.py
@@ -20,7 +20,8 @@
 OWNERS = 8
 EACH = 2
 SLOT = 16
-A_ORDER = (0, 7, 1, 6, 2, 5, 3, 4)
+LATE_OWNERS = (0, 1, 2, 3)
+EARLY_OWNERS = (7, 6, 5, 4)
 B_ORDER = (0, 1, 2, 3, 4, 5, 6, 7, 15, 14, 13, 12, 8, 9, 10, 11)
 
 
@@ -344,12 +345,19 @@
         )
 
     pl.semaphore_wait(far_sem, 2)
-    for c in A_ORDER:
-        pl.when(me != owners[c])(to_owner(c, me).start)
-
-        @pl.when(me == owners[c])
+    def hand_over(c, going):
+        pl.when(going & (me != owners[c]))(to_owner(c, me).start)
+
+        @pl.when(going & (me == owners[c]))
         def _():
             recv_a[rows(me, 6 * EACH + 1), :] = send_a[rows(c, 6 * EACH + 1), :]
+
+    for c in LATE_OWNERS:
+        hand_over(c, me < nx // 2)
+    for c in EARLY_OWNERS:
+        hand_over(c, me >= 0)
+    for c in LATE_OWNERS:
+        hand_over(c, me >= nx // 2)
 
     for copy in raw_y + raw_z:
         copy.wait_recv()

time: 31.2 us -> 31.1 us (level)
  no operation moved by 1% of the time
where the time goes in v5:
time: 31.1 us; the launch traced here: 31 us
  Pallas kernels  31 us (100%)
    pallas_call x1, Pallas kernels, on_device(): pl.pallas_call(functools.partial(solve_kernel, counts), out_shape=(jax.Sh...  30 us
    pallas_call x1, Pallas kernels, on_device(): pl.pallas_call(combine_kernel, out_shape=jax.ShapeDtypeStruct(block, f32)...  0.94 us

profile of v5, /device:TPU:24, one launch (start us, length us, event | category | flops | bytes accessed | tf_op | source)
XLA Modules:
  0.0 31.0 jit_solution(8523559427239976232)
XLA Ops:
  0.0 30.0 %solve.1 = (f32[3,32,16,128]{3,2,1,0:T(8,128)S(1)}, f32[2,32,8,128]{3,2,1,0:T(8,128)S(1)}, f32[2,3,16,128]{3,2,1,0:T(8,128)S(1)}) custom-call(f32[32,16,128]{2,1,0:T(8,128)} %density.1, f32[2,32,16,128]{3,2,1,0:T(8,128)} %momentum.1, f32[32]{0:T(128)} %face.1), custom_call_target="tpu_custom_call" | custom-call | tf_op jit(solution)/shard_map/solve/pallas_call | solution.py:443
  30.0 0.9 %combine.1 = f32[3,32,16,128]{3,2,1,0:T(8,128)} custom-call(f32[3,32,16,128]{3,2,1,0:T(8,128)S(1)} %get-tuple-element.8.local, f32[2,32,8,128]{3,2,1,0:T(8,128)S(1)} %get-tuple-element.9.phi, f32[2,3,16,128]{3,2,1,0:T(8,128)S(1)} %get-tuple-element.10.ends), custom_call_target="tpu_custom_call" | custom-call | tf_op jit(solution)/shard_map/combine/pallas_call | solution.py:484
